TPU v7x, 256 devices: a whole 4x4x8 slice. The times are simulated.
256 devices in a mesh: hi: 8 (over y, core), lo: 32 (over x, z).
Axes of the slice: x: 4, y: 4, z: 8, core: 2. Of those that a mesh axis runs over, the one named last changes fastest.
Arguments:
- vectors: bfloat16 [128, 524288], P(None, ('hi', 'lo')), may hold values from -6 to 6
- leaves: bfloat16 [524288, 512], P(('hi', 'lo')), may hold values from -0.25 to 0.25
- u_local: bfloat16 [2, 524288, 128], P(None, ('hi', 'lo')), may hold values from -0.5 to 0.5
- v_local: bfloat16 [2, 524288, 128], P(None, ('hi', 'lo')), may hold values from -6 to 6
- u_upper: bfloat16 [8, 524288, 128], P(None, ('hi', 'lo')), may hold values from -0.5 to 0.5
- v_upper: bfloat16 [8, 524288, 128], P(None, ('hi', 'lo')), may hold values from -6 to 6
Outputs:
- krylov_last: bfloat16 [128, 524288], P(None, ('hi', 'lo'))
All inputs are finite; a program needn't handle non-finite values.
Results may differ from a plain program's by a relative error of at most 0.018.
Values sent between devices are 32-bit elements; how exact they have to be, the bound alone decides.
No kernel may reach another device: no remote copies, remote signals or barrier semaphores. Data moves between devices by JAX's collectives and lax.ppermute only.
A program may use at most 64 MiB of HBM per device.

v0:
```python
import functools
import math

import jax
import jax.numpy as jnp
from jax import lax
from jax.experimental import pallas as pl
from jax.experimental.pallas import tpu as pltpu
from jax.sharding import PartitionSpec as P

ITERS = 4
TILE = 512
NT = (((1,), (1,)), ((), ()))
VMEM = pl.BlockSpec(memory_space=pltpu.VMEM)


def dot(a, b):
    return jnp.dot(a, b, preferred_element_type=jnp.float32)


def dot_nt(a, b):
    return lax.dot_general(a, b, NT, preferred_element_type=jnp.float32)


def sibling(index):
    return index + 1 - 2 * (index % 2)


def place():
    lo = lax.axis_index("lo")
    half = lo % 2
    return half, 2 * half + (lax.div(lo, 2) + lax.div(lo, 4)) % 2


def section(index, rows):
    return pl.ds(pl.multiple_of(index * rows, rows), rows)


def quarters_of(quarter):
    return (quarter + 2) % 4, sibling(quarter), 3 - quarter, quarter


def project(state_ref, v_ref, outs, parts_ref):
    sends, keep_ref, early, early_keep_ref = outs[:3], outs[3], outs[4:7], outs[7]
    own_half, own_quarter = place()
    wide = state_ref.shape[0]
    half, quarter = wide // 2, wide // 4
    levels, _, rank = v_ref.shape

    def two_levels(pair, _):
        level = 2 * pair
        both = dot(state_ref[...], jnp.concatenate([v_ref[level], v_ref[level + 1]], axis=1))
        parts_ref[level] = both[:, :rank]
        parts_ref[level + 1] = both[:, rank:]
        return 0

    lax.fori_loop(0, levels // 2, two_levels, 0)
    early[0][pl.ds(0, wide), :] = parts_ref[0]
    early[1][pl.ds(0, half), :] = parts_ref[1, section(own_half, half), :]
    early[2][pl.ds(0, half), :] = parts_ref[1, section(1 - own_half, half), :]
    targets = ((early[0], wide), (early[1], half), (early[2], half), (early_keep_ref, 0))
    places = quarters_of(own_quarter)
    for (ref, start), index in zip(targets, places):
        ref[pl.ds(start, quarter), :] = parts_ref[2, section(index, quarter), :]
    for level in range(3, levels):
        for ref, index in zip((*sends, keep_ref), places):
            ref[pl.ds((level - 3) * quarter, quarter), :] = parts_ref[level, section(index, quarter), :]


def first_kernel(state_ref, v_ref, *refs):
    *outs, parts_ref = refs
    project(state_ref, v_ref, outs, parts_ref)


def expand(scales, zero_ref, own_ref, near_ref, next_ref, far_ref, base_ref, u_ref, state_ref, coefs_ref):
    wide = base_ref.shape[0]
    half, quarter = wide // 2, wide // 4
    levels, _, rank = u_ref.shape
    own_half, own_quarter = place()

    def put(level, rows, value):
        coefs_ref[rows, pl.ds(level * rank, rank)] = (value * scales[level]).astype(jnp.bfloat16)

    put(0, pl.ds(0, wide), zero_ref[pl.ds(0, wide), :])
    put(1, section(own_half, half), own_ref[pl.ds(0, half), :])
    put(1, section(1 - own_half, half), near_ref[pl.ds(0, half), :])
    for i in range(levels - 2):
        sources = ((near_ref, half), (next_ref, 0), (far_ref, 0), (own_ref, half))
        for (ref, start), index in zip(sources, quarters_of(own_quarter)):
            put(i + 2, section(index, quarter), ref[pl.ds(start + i * quarter, quarter), :])

    def tile(index, _):
        rows = section(index, TILE)
        bases = jnp.concatenate([u_ref[i, rows, :] for i in range(levels)], axis=1)
        state_ref[:, rows] = (base_ref[:, rows] + dot_nt(coefs_ref[...], bases)).astype(jnp.bfloat16)
        return 0

    lax.fori_loop(0, state_ref.shape[1] // TILE, tile, 0)


def middle_kernel(scales, zero, own, near, next_, far, base, u_ref, v_ref, state_ref, *refs):
    *outs, coefs_ref, parts_ref = refs
    expand(scales, zero, own, near, next_, far, base, u_ref, state_ref, coefs_ref)
    project(state_ref, v_ref, outs, parts_ref)


def last_kernel(scales, *refs):
    expand(scales, *refs)


def local_kernel(scales, state_ref, leaves_ref, u_ref, v_ref, base_ref, coefs_ref):
    dev_rows, leaf = leaves_ref.shape
    levels = u_ref.shape[0]
    for level in range(levels):
        size = leaf * 2**level

        def one_node(index, _):
            rows = section(index, size)
            coefs_ref[level, index] = (dot(state_ref[:, rows], v_ref[level, rows, :]) * scales[level]).astype(
                jnp.bfloat16
            )
            return 0

        lax.fori_loop(0, dev_rows // size, one_node, 0)

    def one_leaf(index, _):
        rows = section(index, leaf)
        left = [state_ref[:, rows]]
        right = [leaves_ref[rows, :]]
        for level in range(levels):
            left.append(coefs_ref[level, sibling(lax.div(index, 2**level))])
            right.append(u_ref[level, rows, :])
        base_ref[:, rows] = dot_nt(jnp.concatenate(left, axis=1), jnp.concatenate(right, axis=1))
        return 0

    lax.fori_loop(0, dev_rows // leaf, one_leaf, 0)


def four_kernel(keep_ref, near_ref, next_ref, far_ref, out_ref):
    out_ref[...] = (keep_ref[...] + near_ref[...]) + (next_ref[...] + far_ref[...])


def line_kernel(arrived_ref, kept_ref, *refs):
    early, (out_ref, *late) = refs[:3], refs[3:]
    out_ref[...] = kept_ref[...] + arrived_ref[...]
    for source, target in zip(early, late):
        target[...] = source[...]


def early_kernel(keep_ref, near_ref, next_ref, far_ref, one_ref, two_ref):
    half, quarter = one_ref.shape[0], two_ref.shape[0]
    skip = near_ref.shape[0] - quarter
    one_ref[...] = next_ref[pl.ds(0, half), :] + far_ref[pl.ds(0, half), :]
    two_ref[...] = (keep_ref[...] + near_ref[pl.ds(skip, quarter), :]) + (
        next_ref[pl.ds(half, quarter), :] + far_ref[pl.ds(half, quarter), :]
    )


def add_kernel(arrived_ref, kept_ref, *refs):
    out_ref = refs[-1]
    rows = out_ref.shape[0]
    out_ref[...] = (
        kept_ref[pl.ds(kept_ref.shape[0] - rows, rows), :]
        + arrived_ref[pl.ds(arrived_ref.shape[0] - rows, rows), :]
    )


def join_kernel(one_ref, *refs):
    *pieces, long_ref, short_ref = refs
    half = one_ref.shape[0]
    rows = pieces[-1].shape[0]
    long_ref[pl.ds(0, half), :] = one_ref[...]
    for i, ref in enumerate(pieces):
        piece = ref[pl.ds(0, rows), :]
        long_ref[pl.ds(half + i * rows, rows), :] = piece
        short_ref[pl.ds(i * rows, rows), :] = piece


def call(kernel, name, outs, *args, scratch=()):
    return pl.pallas_call(
        kernel,
        out_shape=outs,
        in_specs=[VMEM] * len(args),
        out_specs=jax.tree.map(lambda _: VMEM, outs),
        scratch_shapes=scratch,
        compiler_params=pltpu.CompilerParams(vmem_limit_bytes=6 * 2**20),
        name=name,
    )(*args)


def stack(rows, rank):
    return jax.ShapeDtypeStruct((rows, rank), jnp.float32)


def from_partner(value, axis, mask):
    pairs = [(source, source ^ mask) for source in range(lax.axis_size(axis))]
    return lax.ppermute(value, axis, pairs)


def exchange(parts):
    sends, keep, early, early_keep = parts[:3], parts[3], parts[4:7], parts[7]
    rows, rank = keep.shape
    quarter = early_keep.shape[0]
    half = 2 * quarter
    masks = (1, 2, 3)
    arrived = [from_partner(send, "lo", mask) for send, mask in zip(sends, masks)]
    total = call(four_kernel, "four", stack(rows, rank), keep, *arrived)
    shapes = (stack(rows, rank), *(stack(send.shape[0], rank) for send in early))
    total, *early = call(line_kernel, "line", shapes, from_partner(total, "lo", 6), total, *early)
    early = [from_partner(send, "lo", mask) for send, mask in zip(early, masks)]
    one, two = call(early_kernel, "early", (stack(half, rank), stack(quarter, rank)), early_keep, *early)
    found = [from_partner(two, "lo", 6)]
    for axis, mask in (("lo", 8), ("lo", 24), ("hi", 1), ("hi", 2), ("hi", 6)):
        value = from_partner(total, axis, mask)
        found.append(value)
        rows = total.shape[0] - quarter
        if rows:
            ahead = (two,) if (axis, mask) == ("hi", 2) else ()
            total = call(add_kernel, "add", stack(rows, rank), value, total, *ahead)
    rows = len(found) * quarter
    long, short = call(join_kernel, "join", (stack(half + rows, rank), stack(rows, rank)), one, *found)
    return early[0], long, from_partner(long, "lo", 1), from_partner(short, "lo", 2), from_partner(short, "lo", 3)


def local(vectors, leaves, u_local, v_local, u_upper, v_upper):
    wide, dev_rows = vectors.shape
    leaf = leaves.shape[1]
    rank = u_local.shape[2]
    local_count = u_local.shape[0]
    upper_count = u_upper.shape[0]
    level_count = local_count + upper_count
    scales = [1.0 / math.sqrt(leaf * 2**level * level_count) for level in range(level_count)]
    upper_scales = scales[local_count:]
    half, quarter = wide // 2, wide // 4
    upper = (upper_count - 3) * quarter
    rows = [upper] * 4 + [wide + quarter, half + quarter, half + quarter, quarter]
    part_shapes = tuple(stack(number, rank) for number in rows)
    state_shape = jax.ShapeDtypeStruct((wide, dev_rows), jnp.bfloat16)
    base_shape = jax.ShapeDtypeStruct((wide, dev_rows), jnp.float32)
    part_scratch = [pltpu.VMEM((upper_count, wide, rank), jnp.float32)]
    coef_scratch = [pltpu.VMEM((wide, upper_count * rank), jnp.bfloat16)]
    local_scratch = [pltpu.VMEM((local_count, dev_rows // leaf, wide, rank), jnp.bfloat16)]
    state = vectors
    parts = call(first_kernel, "first", part_shapes, state, v_upper, scratch=part_scratch)

    def found(state, parts):
        base = call(
            functools.partial(local_kernel, scales[:local_count]), "local", base_shape, state, leaves, u_local, v_local,
            scratch=local_scratch,
        )
        return *exchange(parts), base

    def step(_, carry):
        state, *parts = carry
        return tuple(
            call(
                functools.partial(middle_kernel, upper_scales), "middle", (state_shape, *part_shapes),
                *found(state, parts), u_upper, v_upper, scratch=coef_scratch + part_scratch,
            )
        )

    state, *parts = lax.fori_loop(0, ITERS - 1, step, (state, *parts))
    return call(
        functools.partial(last_kernel, upper_scales), "last", state_shape, *found(state, parts), u_upper,
        scratch=coef_scratch,
    )


def solution(mesh):
    return jax.shard_map(
        local,
        mesh=mesh,
        in_specs=(
            P(None, ("hi", "lo")),
            P(("hi", "lo"), None),
            P(None, ("hi", "lo"), None),
            P(None, ("hi", "lo"), None),
            P(None, ("hi", "lo"), None),
            P(None, ("hi", "lo"), None),
        ),
        out_specs=P(None, ("hi", "lo")),
        check_vma=False,
    )
```

profile of v0, /device:TPU:6, one launch (start us, length us, event | category | flops | bytes accessed | tf_op | source)
XLA Modules:
  0.0 238.5 jit_solution(5262244551083018349)
XLA Ops:
  1.2 4.1 %first.1 = (f32[160,128]{1,0:T(8,128)}, f32[160,128]{1,0:T(8,128)}, f32[160,128]{1,0:T(8,128)}, f32[160,128]{1,0:T(8,128)S(1)}, f32[160,128]{1,0:T(8,128)S(1)}, ...) custom-call(bf16[128,2048]{1,0:T(8,128)(2,1)S(1)} %copy.39.state_ref, bf16[8,2048,128]{2,1,0:T(8,128)(2,1)} %v_ref.2), custom_call_target="tpu_custom_call" | custom-call | tf_op jit(solution)/shard_map/first/pallas_call | solution.py:180
  5.3 178.9 %while.26 = (s32[]{:T(128)}, bf16[128,2048]{1,0:T(8,128)(2,1)S(1)}, f32[160,128]{1,0:T(8,128)}, f32[160,128]{1,0:T(8,128)}, f32[160,128]{1,0:T(8,128)}, /*index=...) while((s32[]{:T(128)}, bf16[128,2048]{1,0:T(8,128)(2,1)S(1)}, ...), condition=%wide.region_1.0_spmd, body=%wide.region_0.0_spmd.sunk | while | flops 2 | bytes 21168944 | solution.py:262
  5.3 4.6 %collective-permute-start.2 = (f32[160,128]{1,0:T(8,128)}, f32[160,128]{1,0:T(8,128)S(1)}, u32[]{:S(2)}, u32[]{:S(2)}) collective-permute-start(f32[160,128]{1,0:T(8,128)} %get-tuple-element.323), channel_id=1, source_target_pairs={{0,3},{1,2},{2,1},{3,0},{4,7},{5,6},{6,5},{7,4},{8,11},{9,10},{10,... | collective-permute-start | bytes 245768 | tf_op jit(solution)/shard_map/while/body/eval_jaxpr/ppermute | solution.py:197
  10.6 2.9 %collective-permute-done.2.far_ref = f32[160,128]{1,0:T(8,128)S(1)} collective-permute-done((f32[160,128]{1,0:T(8,128)}, f32[160,128]{1,0:T(8,128)S(1)}, u32[]{:S(2)}, u32[]{:S(2)}) %collective-permute-start.2) | collective-permute-done | bytes 81952 | tf_op jit(solution)/shard_map/while/body/eval_jaxpr/ppermute | solution.py:197
  13.5 3.1 %collective-permute-done.1.next_ref = f32[160,128]{1,0:T(8,128)S(1)} collective-permute-done((f32[160,128]{1,0:T(8,128)}, f32[160,128]{1,0:T(8,128)S(1)}, u32[]{:S(2)}, u32[]{:S(2)}) %collective-permute-start.1) | collective-permute-done | bytes 81952 | tf_op jit(solution)/shard_map/while/body/eval_jaxpr/ppermute | solution.py:197
  16.6 4.0 %collective-permute-start.3 = (f32[160,128]{1,0:T(8,128)S(1)}, f32[160,128]{1,0:T(8,128)S(1)}, u32[]{:S(2)}, u32[]{:S(2)}) collective-permute-start(f32[160,128]{1,0:T(8,128)S(1)} %four.3.kept_ref), channel_id=1, source_target_pairs={{0,6},{1,7},{2,4},{3,5},{4,2},{5,3},{6,0},{7,1},{8,14},{9,15},{10,... | collective-permute-start | bytes 245768 | tf_op jit(solution)/shard_map/while/body/eval_jaxpr/ppermute | solution.py:197
  20.6 2.9 %collective-permute-done.3.arrived_ref = f32[160,128]{1,0:T(8,128)S(1)} collective-permute-done((f32[160,128]{1,0:T(8,128)S(1)}, f32[160,128]{1,0:T(8,128)S(1)}, u32[]{:S(2)}, u32[]{:S(2)}) %collective-permute-start.3) | collective-permute-done | bytes 81952 | tf_op jit(solution)/shard_map/while/body/eval_jaxpr/ppermute | solution.py:197
  24.4 3.6 %collective-permute-done.8.arrived_ref.refs_1_ = f32[160,128]{1,0:T(8,128)S(1)} collective-permute-done((f32[160,128]{1,0:T(8,128)S(1)}, f32[160,128]{1,0:T(8,128)S(1)}, u32[]{:S(2)}, u32[]{:S(2)}) %collective-permute-start.8) | collective-permute-done | bytes 81952 | tf_op jit(solution)/shard_map/while/body/eval_jaxpr/ppermute | solution.py:197
  28.6 2.9 %collective-permute-start.4 = (f32[160,128]{1,0:T(8,128)S(1)}, f32[160,128]{1,0:T(8,128)S(1)}, u32[]{:S(2)}, u32[]{:S(2)}) collective-permute-start(f32[160,128]{1,0:T(8,128)S(1)} %get-tuple-element.286), channel_id=1, source_target_pairs={{0,1},{1,0},{2,3},{3,2},{4,5},{5,4},{6,7},{7,6},{8,9},{9,8},{10,11... | collective-permute-start | bytes 245768 | tf_op jit(solution)/shard_map/while/body/eval_jaxpr/ppermute | solution.py:197
  31.5 2.1 collective-permute-done.9.arrived_ref.refs_2_
  33.7 3.9 %collective-permute-start.5 = (f32[96,128]{1,0:T(8,128)S(1)}, f32[96,128]{1,0:T(8,128)S(1)}, u32[]{:S(2)}, u32[]{:S(2)}) collective-permute-start(f32[96,128]{1,0:T(8,128)S(1)} %get-tuple-element.287), channel_id=1, source_target_pairs={{0,2},{1,3},{2,0},{3,1},{4,6},{5,7},{6,4},{7,5},{8,10},{9,11},{10,... | collective-permute-start | bytes 147464 | tf_op jit(solution)/shard_map/while/body/eval_jaxpr/ppermute | solution.py:197
  41.3 2.2 collective-permute-done.6.far_ref
  43.5 3.1 %collective-permute-start.7 = (f32[32,128]{1,0:T(8,128)S(1)}, f32[32,128]{1,0:T(8,128)S(1)}, u32[]{:S(2)}, u32[]{:S(2)}) collective-permute-start(f32[32,128]{1,0:T(8,128)S(1)} %get-tuple-element.290.refs_0_), channel_id=1, source_target_pairs={{0,6},{1,7},{2,4},{3,5},{4,2},{5,3},{6,0},{7,1},{8,14},{9,15},{10,... | collective-permute-start | bytes 49160 | tf_op jit(solution)/shard_map/while/body/eval_jaxpr/ppermute | solution.py:197
  46.6 3.1 %collective-permute-start.12 = (f32[32,128]{1,0:T(8,128)S(1)}, f32[32,128]{1,0:T(8,128)S(1)}, u32[]{:S(2)}, u32[]{:S(2)}) collective-permute-start(f32[32,128]{1,0:T(8,128)S(1)} %add.20), channel_id=1, source_target_pairs={{0,192},{32,224},{64,128},{96,160},{128,64},{160,96},{192,0},{224,... | collective-permute-start | bytes 49160 | tf_op jit(solution)/shard_map/while/body/eval_jaxpr/ppermute | solution.py:197
  49.7 1.9 collective-permute-done.12.refs_5_
  52.2 1.9 collective-permute-start.15
  55.2 4.4 %local.3.base = f32[128,2048]{1,0:T(8,128)S(1)} custom-call(bf16[128,2048]{1,0:T(8,128)(2,1)S(1)} %get-tuple-element.320.state_ref, bf16[2048,512]{1,0:T(8,128)(2,1)S(1)} %get-tuple-element.345.leaves_ref, bf16[2,2048,128]{2,1,0:T(8,128)(2,1)} %get-tuple-element.346.u_ref, bf16[2,2048,128]{2,1,0:T(8,128)(2,1)} %get-tuple-element.347.v_ref), custom_call_target="tpu_custom_call" | custom-call | tf_op jit(solution)/shard_map/while/body/eval_jaxpr/local/pallas_call | solution.py:180
  59.6 3.0 %collective-permute-done.14.next_ = f32[192,128]{1,0:T(8,128)S(1)} collective-permute-done((f32[192,128]{1,0:T(8,128)S(1)}, f32[192,128]{1,0:T(8,128)S(1)}, u32[]{:S(2)}, u32[]{:S(2)}) %collective-permute-start.14) | collective-permute-done | bytes 98336 | tf_op jit(solution)/shard_map/while/body/eval_jaxpr/ppermute | solution.py:197
  62.6 6.1 %middle.1 = (bf16[128,2048]{1,0:T(8,128)(2,1)S(1)}, f32[160,128]{1,0:T(8,128)}, f32[160,128]{1,0:T(8,128)}, f32[160,128]{1,0:T(8,128)}, f32[160,128]{1,0:T(8,128...) custom-call(f32[160,128]{1,0:T(8,128)S(1)} %collective-permute-done.4.nea, ...), custom_call_target="tpu_custom_call" | custom-call | tf_op jit(solution)/shard_map/while/body/eval_jaxpr/middle/pallas_call | solution.py:180
  68.8 1.9 collective-permute-start.2
  70.7 2.5 %collective-permute-start = (f32[160,128]{1,0:T(8,128)}, f32[160,128]{1,0:T(8,128)S(1)}, u32[]{:S(2)}, u32[]{:S(2)}) collective-permute-start(f32[160,128]{1,0:T(8,128)} %get-tuple-element.321), channel_id=1, source_target_pairs={{0,1},{1,0},{2,3},{3,2},{4,5},{5,4},{6,7},{7,6},{8,9},{9,8},{10,11... | collective-permute-start | bytes 245768 | tf_op jit(solution)/shard_map/while/body/eval_jaxpr/ppermute | solution.py:197
  73.1 2.4 collective-permute-done.2.far_ref
  75.5 2.1 collective-permute-done.1.next_ref
  78.4 5.9 %collective-permute-done.3.arrived_ref = f32[160,128]{1,0:T(8,128)S(1)} collective-permute-done((f32[160,128]{1,0:T(8,128)S(1)}, f32[160,128]{1,0:T(8,128)S(1)}, u32[]{:S(2)}, u32[]{:S(2)}) %collective-permute-start.3) | collective-permute-done | bytes 81952 | tf_op jit(solution)/shard_map/while/body/eval_jaxpr/ppermute | solution.py:197
  84.4 4.4 %collective-permute-done.8.arrived_ref.refs_1_ = f32[160,128]{1,0:T(8,128)S(1)} collective-permute-done((f32[160,128]{1,0:T(8,128)S(1)}, f32[160,128]{1,0:T(8,128)S(1)}, u32[]{:S(2)}, u32[]{:S(2)}) %collective-permute-start.8) | collective-permute-done | bytes 81952 | tf_op jit(solution)/shard_map/while/body/eval_jaxpr/ppermute | solution.py:197
  89.4 1.9 collective-permute-start.4
  91.3 3.1 %collective-permute-done.9.arrived_ref.refs_2_ = f32[128,128]{1,0:T(8,128)S(1)} collective-permute-done((f32[128,128]{1,0:T(8,128)S(1)}, f32[128,128]{1,0:T(8,128)S(1)}, u32[]{:S(2)}, u32[]{:S(2)}) %collective-permute-start.9) | collective-permute-done | bytes 65568 | tf_op jit(solution)/shard_map/while/body/eval_jaxpr/ppermute | solution.py:197
  94.5 2.4 %collective-permute-start.5 = (f32[96,128]{1,0:T(8,128)S(1)}, f32[96,128]{1,0:T(8,128)S(1)}, u32[]{:S(2)}, u32[]{:S(2)}) collective-permute-start(f32[96,128]{1,0:T(8,128)S(1)} %get-tuple-element.287), channel_id=1, source_target_pairs={{0,2},{1,3},{2,0},{3,1},{4,6},{5,7},{6,4},{7,5},{8,10},{9,11},{10,... | collective-permute-start | bytes 147464 | tf_op jit(solution)/shard_map/while/body/eval_jaxpr/ppermute | solution.py:197
  96.9 1.9 collective-permute-start.6
  99.9 2.9 %collective-permute-done.6.far_ref = f32[96,128]{1,0:T(8,128)S(1)} collective-permute-done((f32[96,128]{1,0:T(8,128)S(1)}, f32[96,128]{1,0:T(8,128)S(1)}, u32[]{:S(2)}, u32[]{:S(2)}) %collective-permute-start.6) | collective-permute-done | bytes 49184 | tf_op jit(solution)/shard_map/while/body/eval_jaxpr/ppermute | solution.py:197
  104.0 3.1 %collective-permute-start.12 = (f32[32,128]{1,0:T(8,128)S(1)}, f32[32,128]{1,0:T(8,128)S(1)}, u32[]{:S(2)}, u32[]{:S(2)}) collective-permute-start(f32[32,128]{1,0:T(8,128)S(1)} %add.20), channel_id=1, source_target_pairs={{0,192},{32,224},{64,128},{96,160},{128,64},{160,96},{192,0},{224,... | collective-permute-start | bytes 49160 | tf_op jit(solution)/shard_map/while/body/eval_jaxpr/ppermute | solution.py:197
  110.5 2.0 collective-permute-start.15
  112.6 4.4 %local.3.base = f32[128,2048]{1,0:T(8,128)S(1)} custom-call(bf16[128,2048]{1,0:T(8,128)(2,1)S(1)} %get-tuple-element.320.state_ref, bf16[2048,512]{1,0:T(8,128)(2,1)S(1)} %get-tuple-element.345.leaves_ref, bf16[2,2048,128]{2,1,0:T(8,128)(2,1)} %get-tuple-element.346.u_ref, bf16[2,2048,128]{2,1,0:T(8,128)(2,1)} %get-tuple-element.347.v_ref), custom_call_target="tpu_custom_call" | custom-call | tf_op jit(solution)/shard_map/while/body/eval_jaxpr/local/pallas_call | solution.py:180
  117.2 2.7 %collective-permute-done.14.next_ = f32[192,128]{1,0:T(8,128)S(1)} collective-permute-done((f32[192,128]{1,0:T(8,128)S(1)}, f32[192,128]{1,0:T(8,128)S(1)}, u32[]{:S(2)}, u32[]{:S(2)}) %collective-permute-start.14) | collective-permute-done | bytes 98336 | tf_op jit(solution)/shard_map/while/body/eval_jaxpr/ppermute | solution.py:197
  119.9 6.1 %middle.1 = (bf16[128,2048]{1,0:T(8,128)(2,1)S(1)}, f32[160,128]{1,0:T(8,128)}, f32[160,128]{1,0:T(8,128)}, f32[160,128]{1,0:T(8,128)}, f32[160,128]{1,0:T(8,128...) custom-call(f32[160,128]{1,0:T(8,128)S(1)} %collective-permute-done.4.nea, ...), custom_call_target="tpu_custom_call" | custom-call | tf_op jit(solution)/shard_map/while/body/eval_jaxpr/middle/pallas_call | solution.py:180
  126.0 2.2 collective-permute-start.2
  128.2 2.2 collective-permute-start
  130.4 2.9 %collective-permute-done.2.far_ref = f32[160,128]{1,0:T(8,128)S(1)} collective-permute-done((f32[160,128]{1,0:T(8,128)}, f32[160,128]{1,0:T(8,128)S(1)}, u32[]{:S(2)}, u32[]{:S(2)}) %collective-permute-start.2) | collective-permute-done | bytes 81952 | tf_op jit(solution)/shard_map/while/body/eval_jaxpr/ppermute | solution.py:197
  134.9 1.9 collective-permute-start.3
  136.9 4.7 %collective-permute-done.3.arrived_ref = f32[160,128]{1,0:T(8,128)S(1)} collective-permute-done((f32[160,128]{1,0:T(8,128)S(1)}, f32[160,128]{1,0:T(8,128)S(1)}, u32[]{:S(2)}, u32[]{:S(2)}) %collective-permute-start.3) | collective-permute-done | bytes 81952 | tf_op jit(solution)/shard_map/while/body/eval_jaxpr/ppermute | solution.py:197
  141.7 4.4 %collective-permute-done.8.arrived_ref.refs_1_ = f32[160,128]{1,0:T(8,128)S(1)} collective-permute-done((f32[160,128]{1,0:T(8,128)S(1)}, f32[160,128]{1,0:T(8,128)S(1)}, u32[]{:S(2)}, u32[]{:S(2)}) %collective-permute-start.8) | collective-permute-done | bytes 81952 | tf_op jit(solution)/shard_map/while/body/eval_jaxpr/ppermute | solution.py:197
  146.9 4.8 %collective-permute-done.9.arrived_ref.refs_2_ = f32[128,128]{1,0:T(8,128)S(1)} collective-permute-done((f32[128,128]{1,0:T(8,128)S(1)}, f32[128,128]{1,0:T(8,128)S(1)}, u32[]{:S(2)}, u32[]{:S(2)}) %collective-permute-start.9) | collective-permute-done | bytes 65568 | tf_op jit(solution)/shard_map/while/body/eval_jaxpr/ppermute | solution.py:197
  151.8 2.5 %collective-permute-start.5 = (f32[96,128]{1,0:T(8,128)S(1)}, f32[96,128]{1,0:T(8,128)S(1)}, u32[]{:S(2)}, u32[]{:S(2)}) collective-permute-start(f32[96,128]{1,0:T(8,128)S(1)} %get-tuple-element.287), channel_id=1, source_target_pairs={{0,2},{1,3},{2,0},{3,1},{4,6},{5,7},{6,4},{7,5},{8,10},{9,11},{10,... | collective-permute-start | bytes 147464 | tf_op jit(solution)/shard_map/while/body/eval_jaxpr/ppermute | solution.py:197
  154.9 2.6 %collective-permute-done.5.next_ref = f32[96,128]{1,0:T(8,128)S(1)} collective-permute-done((f32[96,128]{1,0:T(8,128)S(1)}, f32[96,128]{1,0:T(8,128)S(1)}, u32[]{:S(2)}, u32[]{:S(2)}) %collective-permute-start.5) | collective-permute-done | bytes 49184 | tf_op jit(solution)/shard_map/while/body/eval_jaxpr/ppermute | solution.py:197
  157.5 2.6 %collective-permute-done.6.far_ref = f32[96,128]{1,0:T(8,128)S(1)} collective-permute-done((f32[96,128]{1,0:T(8,128)S(1)}, f32[96,128]{1,0:T(8,128)S(1)}, u32[]{:S(2)}, u32[]{:S(2)}) %collective-permute-start.6) | collective-permute-done | bytes 49184 | tf_op jit(solution)/shard_map/while/body/eval_jaxpr/ppermute | solution.py:197
  160.2 2.2 collective-permute-start.7
  162.4 3.1 %collective-permute-start.12 = (f32[32,128]{1,0:T(8,128)S(1)}, f32[32,128]{1,0:T(8,128)S(1)}, u32[]{:S(2)}, u32[]{:S(2)}) collective-permute-start(f32[32,128]{1,0:T(8,128)S(1)} %add.20), channel_id=1, source_target_pairs={{0,192},{32,224},{64,128},{96,160},{128,64},{160,96},{192,0},{224,... | collective-permute-start | bytes 49160 | tf_op jit(solution)/shard_map/while/body/eval_jaxpr/ppermute | solution.py:197
  168.8 1.9 collective-permute-start.15
  171.0 4.4 %local.3.base = f32[128,2048]{1,0:T(8,128)S(1)} custom-call(bf16[128,2048]{1,0:T(8,128)(2,1)S(1)} %get-tuple-element.320.state_ref, bf16[2048,512]{1,0:T(8,128)(2,1)S(1)} %get-tuple-element.345.leaves_ref, bf16[2,2048,128]{2,1,0:T(8,128)(2,1)} %get-tuple-element.346.u_ref, bf16[2,2048,128]{2,1,0:T(8,128)(2,1)} %get-tuple-element.347.v_ref), custom_call_target="tpu_custom_call" | custom-call | tf_op jit(solution)/shard_map/while/body/eval_jaxpr/local/pallas_call | solution.py:180
  175.4 2.7 %collective-permute-done.14.next_ = f32[192,128]{1,0:T(8,128)S(1)} collective-permute-done((f32[192,128]{1,0:T(8,128)S(1)}, f32[192,128]{1,0:T(8,128)S(1)}, u32[]{:S(2)}, u32[]{:S(2)}) %collective-permute-start.14) | collective-permute-done | bytes 98336 | tf_op jit(solution)/shard_map/while/body/eval_jaxpr/ppermute | solution.py:197
  178.2 6.1 %middle.1 = (bf16[128,2048]{1,0:T(8,128)(2,1)S(1)}, f32[160,128]{1,0:T(8,128)}, f32[160,128]{1,0:T(8,128)}, f32[160,128]{1,0:T(8,128)}, f32[160,128]{1,0:T(8,128...) custom-call(f32[160,128]{1,0:T(8,128)S(1)} %collective-permute-done.4.nea, ...), custom_call_target="tpu_custom_call" | custom-call | tf_op jit(solution)/shard_map/while/body/eval_jaxpr/middle/pallas_call | solution.py:180
  184.3 2.7 %collective-permute-start.17 = (f32[160,128]{1,0:T(8,128)}, f32[160,128]{1,0:T(8,128)S(1)}, u32[]{:S(2)}, u32[]{:S(2)}) collective-permute-start(f32[160,128]{1,0:T(8,128)} %get-tuple-element.133), channel_id=1, source_target_pairs={{0,2},{1,3},{2,0},{3,1},{4,6},{5,7},{6,4},{7,5},{8,10},{9,11},{10,... | collective-permute-start | bytes 245768 | tf_op jit(solution)/shard_map/ppermute | solution.py:197
  188.9 3.1 %collective-permute-done.17.next_ref = f32[160,128]{1,0:T(8,128)S(1)} collective-permute-done((f32[160,128]{1,0:T(8,128)}, f32[160,128]{1,0:T(8,128)S(1)}, u32[]{:S(2)}, u32[]{:S(2)}) %collective-permute-start.17) | collective-permute-done | bytes 81952 | tf_op jit(solution)/shard_map/ppermute | solution.py:197
  195.1 5.3 %collective-permute-done.19.arrived_ref = f32[160,128]{1,0:T(8,128)S(1)} collective-permute-done((f32[160,128]{1,0:T(8,128)S(1)}, f32[160,128]{1,0:T(8,128)S(1)}, u32[]{:S(2)}, u32[]{:S(2)}) %collective-permute-start.19) | collective-permute-done | bytes 81952 | tf_op jit(solution)/shard_map/ppermute | solution.py:197
  200.6 4.4 %collective-permute-done.24.arrived_ref.refs_1_ = f32[160,128]{1,0:T(8,128)S(1)} collective-permute-done((f32[160,128]{1,0:T(8,128)S(1)}, f32[160,128]{1,0:T(8,128)S(1)}, u32[]{:S(2)}, u32[]{:S(2)}) %collective-permute-start.24) | collective-permute-done | bytes 81952 | tf_op jit(solution)/shard_map/ppermute | solution.py:197
  207.2 3.4 %collective-permute-done.25.arrived_ref.refs_2_ = f32[128,128]{1,0:T(8,128)S(1)} collective-permute-done((f32[128,128]{1,0:T(8,128)S(1)}, f32[128,128]{1,0:T(8,128)S(1)}, u32[]{:S(2)}, u32[]{:S(2)}) %collective-permute-start.25) | collective-permute-done | bytes 65568 | tf_op jit(solution)/shard_map/ppermute | solution.py:197
  210.7 2.3 collective-permute-start.21
  214.9 2.4 %collective-permute-done.21.next_ref = f32[96,128]{1,0:T(8,128)S(1)} collective-permute-done((f32[96,128]{1,0:T(8,128)S(1)}, f32[96,128]{1,0:T(8,128)S(1)}, u32[]{:S(2)}, u32[]{:S(2)}) %collective-permute-start.21) | collective-permute-done | bytes 49184 | tf_op jit(solution)/shard_map/ppermute | solution.py:197
  219.3 3.0 %collective-permute-start.28 = (f32[32,128]{1,0:T(8,128)S(1)}, f32[32,128]{1,0:T(8,128)S(1)}, u32[]{:S(2)}, u32[]{:S(2)}) collective-permute-start(f32[32,128]{1,0:T(8,128)S(1)} %add.16), channel_id=1, source_target_pairs={{0,192},{32,224},{64,128},{96,160},{128,64},{160,96},{192,0},{224,... | collective-permute-start | bytes 49160 | tf_op jit(solution)/shard_map/ppermute | solution.py:197
  222.4 2.5 %collective-permute-done.23.refs_0_ = f32[32,128]{1,0:T(8,128)S(1)} collective-permute-done((f32[32,128]{1,0:T(8,128)S(1)}, f32[32,128]{1,0:T(8,128)S(1)}, u32[]{:S(2)}, u32[]{:S(2)}) %collective-permute-start.23) | collective-permute-done | bytes 16416 | tf_op jit(solution)/shard_map/ppermute | solution.py:197
  226.5 1.9 collective-permute-start.31
  228.5 4.3 %local.2.refs_5_ = f32[128,2048]{1,0:T(8,128)S(1)} custom-call(bf16[128,2048]{1,0:T(8,128)(2,1)S(1)} %get-tuple-element.147.state_ref, bf16[2048,512]{1,0:T(8,128)(2,1)S(1)} %get-tuple-element.410, bf16[2,2048,128]{2,1,0:T(8,128)(2,1)} %get-tuple-element.411, bf16[2,2048,128]{2,1,0:T(8,128)(2,1)} %get-tuple-element.412), custom_call_target="tpu_custom_call" | custom-call | tf_op jit(solution)/shard_map/local/pallas_call | solution.py:180
  233.0 2.7 %collective-permute-done.30.refs_3_ = f32[192,128]{1,0:T(8,128)S(1)} collective-permute-done((f32[192,128]{1,0:T(8,128)S(1)}, f32[192,128]{1,0:T(8,128)S(1)}, u32[]{:S(2)}, u32[]{:S(2)}) %collective-permute-start.30) | collective-permute-done | bytes 98336 | tf_op jit(solution)/shard_map/ppermute | solution.py:197
  235.7 2.8 %last.1 = bf16[128,2048]{1,0:T(8,128)(2,1)} custom-call(f32[160,128]{1,0:T(8,128)S(1)} %collective-permute-done.20.near_ref.refs_0_, f32[256,128]{1,0:T(8,128)S(1)} %get-tuple-element.145.refs_1_, f32[256,128]{1,0:T(8,128)S(1)} %collective-permute-done.29.refs_2_, f32[192,128]{1,0:T(8,128)S(1)} %collective-permute-done.30.refs_3_, ...), custom_call_target="tpu_custom_call" | custom-call | tf_op jit(solution)/shard_map/last/pallas_call | solution.py:180
  (117 shorter events, 36.3 us)
Async XLA Ops:
  5.3 8.2 %collective-permute-start.2 = (f32[160,128]{1,0:T(8,128)}, f32[160,128]{1,0:T(8,128)S(1)}, u32[]{:S(2)}, u32[]{:S(2)}) collective-permute-start(f32[160,128]{1,0:T(8,128)} %get-tuple-element.323), channel_id=1, source_target_pairs={{0,3},{1,2},{2,1},{3,0},{4,7},{5,6},{6,5},{7,4},{8,11},{9,10},{10,... | collective-permute-start | bytes 245768 | tf_op jit(solution)/shard_map/while/body/eval_jaxpr/ppermute | solution.py:197
  10.0 6.6 %collective-permute-start.1 = (f32[160,128]{1,0:T(8,128)}, f32[160,128]{1,0:T(8,128)S(1)}, u32[]{:S(2)}, u32[]{:S(2)}) collective-permute-start(f32[160,128]{1,0:T(8,128)} %get-tuple-element.322), channel_id=1, source_target_pairs={{0,2},{1,3},{2,0},{3,1},{4,6},{5,7},{6,4},{7,5},{8,10},{9,11},{10,... | collective-permute-start | bytes 245768 | tf_op jit(solution)/shard_map/while/body/eval_jaxpr/ppermute | solution.py:197
  10.0 6.6 %collective-permute-start = (f32[160,128]{1,0:T(8,128)}, f32[160,128]{1,0:T(8,128)S(1)}, u32[]{:S(2)}, u32[]{:S(2)}) collective-permute-start(f32[160,128]{1,0:T(8,128)} %get-tuple-element.321), channel_id=1, source_target_pairs={{0,1},{1,0},{2,3},{3,2},{4,5},{5,4},{6,7},{7,6},{8,9},{9,8},{10,11... | collective-permute-start | bytes 245768 | tf_op jit(solution)/shard_map/while/body/eval_jaxpr/ppermute | solution.py:197
  16.6 6.8 %collective-permute-start.3 = (f32[160,128]{1,0:T(8,128)S(1)}, f32[160,128]{1,0:T(8,128)S(1)}, u32[]{:S(2)}, u32[]{:S(2)}) collective-permute-start(f32[160,128]{1,0:T(8,128)S(1)} %four.3.kept_ref), channel_id=1, source_target_pairs={{0,6},{1,7},{2,4},{3,5},{4,2},{5,3},{6,0},{7,1},{8,14},{9,15},{10,... | collective-permute-start | bytes 245768 | tf_op jit(solution)/shard_map/while/body/eval_jaxpr/ppermute | solution.py:197
  23.5 4.5 %collective-permute-start.8 = (f32[160,128]{1,0:T(8,128)S(1)}, f32[160,128]{1,0:T(8,128)S(1)}, u32[]{:S(2)}, u32[]{:S(2)}) collective-permute-start(f32[160,128]{1,0:T(8,128)S(1)} %get-tuple-element.291.kept_ref), channel_id=1, source_target_pairs={{0,8},{1,9},{2,10},{3,11},{4,12},{5,13},{6,14},{7,15},{8,0},{9,1},... | collective-permute-start | bytes 245768 | tf_op jit(solution)/shard_map/while/body/eval_jaxpr/ppermute | solution.py:197
  28.0 5.6 %collective-permute-start.9 = (f32[128,128]{1,0:T(8,128)S(1)}, f32[128,128]{1,0:T(8,128)S(1)}, u32[]{:S(2)}, u32[]{:S(2)}) collective-permute-start(f32[128,128]{1,0:T(8,128)S(1)} %add.17.kept_ref), channel_id=1, source_target_pairs={{0,24},{1,25},{2,26},{3,27},{4,28},{5,29},{6,30},{7,31},{8,16},{9,... | collective-permute-start | bytes 196616 | tf_op jit(solution)/shard_map/while/body/eval_jaxpr/ppermute | solution.py:197
  28.6 14.9 %collective-permute-start.4 = (f32[160,128]{1,0:T(8,128)S(1)}, f32[160,128]{1,0:T(8,128)S(1)}, u32[]{:S(2)}, u32[]{:S(2)}) collective-permute-start(f32[160,128]{1,0:T(8,128)S(1)} %get-tuple-element.286), channel_id=1, source_target_pairs={{0,1},{1,0},{2,3},{3,2},{4,5},{5,4},{6,7},{7,6},{8,9},{9,8},{10,11... | collective-permute-start | bytes 245768 | tf_op jit(solution)/shard_map/while/body/eval_jaxpr/ppermute | solution.py:197
  33.6 5.3 %collective-permute-start.10 = (f32[96,128]{1,0:T(8,128)S(1)}, f32[96,128]{1,0:T(8,128)S(1)}, u32[]{:S(2)}, u32[]{:S(2)}) collective-permute-start(f32[96,128]{1,0:T(8,128)S(1)} %add.18.kept_ref), channel_id=1, source_target_pairs={{0,32},{32,0},{64,96},{96,64},{128,160},{160,128},{192,224},{224,1... | collective-permute-start | bytes 147464 | tf_op jit(solution)/shard_map/while/body/eval_jaxpr/ppermute | solution.py:197
  33.7 7.6 %collective-permute-start.5 = (f32[96,128]{1,0:T(8,128)S(1)}, f32[96,128]{1,0:T(8,128)S(1)}, u32[]{:S(2)}, u32[]{:S(2)}) collective-permute-start(f32[96,128]{1,0:T(8,128)S(1)} %get-tuple-element.287), channel_id=1, source_target_pairs={{0,2},{1,3},{2,0},{3,1},{4,6},{5,7},{6,4},{7,5},{8,10},{9,11},{10,... | collective-permute-start | bytes 147464 | tf_op jit(solution)/shard_map/while/body/eval_jaxpr/ppermute | solution.py:197
  37.6 5.9 %collective-permute-start.6 = (f32[96,128]{1,0:T(8,128)S(1)}, f32[96,128]{1,0:T(8,128)S(1)}, u32[]{:S(2)}, u32[]{:S(2)}) collective-permute-start(f32[96,128]{1,0:T(8,128)S(1)} %get-tuple-element.288), channel_id=1, source_target_pairs={{0,3},{1,2},{2,1},{3,0},{4,7},{5,6},{6,5},{7,4},{8,11},{9,10},{10,... | collective-permute-start | bytes 147464 | tf_op jit(solution)/shard_map/while/body/eval_jaxpr/ppermute | solution.py:197
  38.9 7.7 %collective-permute-start.11 = (f32[64,128]{1,0:T(8,128)S(1)}, f32[64,128]{1,0:T(8,128)S(1)}, u32[]{:S(2)}, u32[]{:S(2)}) collective-permute-start(f32[64,128]{1,0:T(8,128)S(1)} %add.19.kept_ref), channel_id=1, source_target_pairs={{0,64},{32,96},{64,0},{96,32},{128,192},{160,224},{192,128},{224,1... | collective-permute-start | bytes 98312 | tf_op jit(solution)/shard_map/while/body/eval_jaxpr/ppermute | solution.py:197
  43.5 6.2 %collective-permute-start.7 = (f32[32,128]{1,0:T(8,128)S(1)}, f32[32,128]{1,0:T(8,128)S(1)}, u32[]{:S(2)}, u32[]{:S(2)}) collective-permute-start(f32[32,128]{1,0:T(8,128)S(1)} %get-tuple-element.290.refs_0_), channel_id=1, source_target_pairs={{0,6},{1,7},{2,4},{3,5},{4,2},{5,3},{6,0},{7,1},{8,14},{9,15},{10,... | collective-permute-start | bytes 49160 | tf_op jit(solution)/shard_map/while/body/eval_jaxpr/ppermute | solution.py:197
  46.6 5.0 %collective-permute-start.12 = (f32[32,128]{1,0:T(8,128)S(1)}, f32[32,128]{1,0:T(8,128)S(1)}, u32[]{:S(2)}, u32[]{:S(2)}) collective-permute-start(f32[32,128]{1,0:T(8,128)S(1)} %add.20), channel_id=1, source_target_pairs={{0,192},{32,224},{64,128},{96,160},{128,64},{160,96},{192,0},{224,... | collective-permute-start | bytes 49160 | tf_op jit(solution)/shard_map/while/body/eval_jaxpr/ppermute | solution.py:197
  51.6 11.0 %collective-permute-start.13 = (f32[256,128]{1,0:T(8,128)S(1)}, f32[256,128]{1,0:T(8,128)S(1)}, u32[]{:S(2)}, u32[]{:S(2)}) collective-permute-start(f32[256,128]{1,0:T(8,128)S(1)} %get-tuple-element.292.own), channel_id=1, source_target_pairs={{0,1},{1,0},{2,3},{3,2},{4,5},{5,4},{6,7},{7,6},{8,9},{9,8},{10,11... | collective-permute-start | bytes 393224 | tf_op jit(solution)/shard_map/while/body/eval_jaxpr/ppermute | solution.py:197
  52.2 7.4 %collective-permute-start.15 = (f32[192,128]{1,0:T(8,128)S(1)}, f32[192,128]{1,0:T(8,128)S(1)}, u32[]{:S(2)}, u32[]{:S(2)}) collective-permute-start(f32[192,128]{1,0:T(8,128)S(1)} %get-tuple-element.293), channel_id=1, source_target_pairs={{0,3},{1,2},{2,1},{3,0},{4,7},{5,6},{6,5},{7,4},{8,11},{9,10},{10,... | collective-permute-start | bytes 294920 | tf_op jit(solution)/shard_map/while/body/eval_jaxpr/ppermute | solution.py:197
  54.1 8.5 %collective-permute-start.14 = (f32[192,128]{1,0:T(8,128)S(1)}, f32[192,128]{1,0:T(8,128)S(1)}, u32[]{:S(2)}, u32[]{:S(2)}) collective-permute-start(f32[192,128]{1,0:T(8,128)S(1)} %get-tuple-element.293), channel_id=1, source_target_pairs={{0,2},{1,3},{2,0},{3,1},{4,6},{5,7},{6,4},{7,5},{8,10},{9,11},{10,... | collective-permute-start | bytes 294920 | tf_op jit(solution)/shard_map/while/body/eval_jaxpr/ppermute | solution.py:197
  68.8 6.8 %collective-permute-start.2 = (f32[160,128]{1,0:T(8,128)}, f32[160,128]{1,0:T(8,128)S(1)}, u32[]{:S(2)}, u32[]{:S(2)}) collective-permute-start(f32[160,128]{1,0:T(8,128)} %get-tuple-element.323), channel_id=1, source_target_pairs={{0,3},{1,2},{2,1},{3,0},{4,7},{5,6},{6,5},{7,4},{8,11},{9,10},{10,... | collective-permute-start | bytes 245768 | tf_op jit(solution)/shard_map/while/body/eval_jaxpr/ppermute | solution.py:197
  70.7 6.9 %collective-permute-start.1 = (f32[160,128]{1,0:T(8,128)}, f32[160,128]{1,0:T(8,128)S(1)}, u32[]{:S(2)}, u32[]{:S(2)}) collective-permute-start(f32[160,128]{1,0:T(8,128)} %get-tuple-element.322), channel_id=1, source_target_pairs={{0,2},{1,3},{2,0},{3,1},{4,6},{5,7},{6,4},{7,5},{8,10},{9,11},{10,... | collective-permute-start | bytes 245768 | tf_op jit(solution)/shard_map/while/body/eval_jaxpr/ppermute | solution.py:197
  70.7 6.9 %collective-permute-start = (f32[160,128]{1,0:T(8,128)}, f32[160,128]{1,0:T(8,128)S(1)}, u32[]{:S(2)}, u32[]{:S(2)}) collective-permute-start(f32[160,128]{1,0:T(8,128)} %get-tuple-element.321), channel_id=1, source_target_pairs={{0,1},{1,0},{2,3},{3,2},{4,5},{5,4},{6,7},{7,6},{8,9},{9,8},{10,11... | collective-permute-start | bytes 245768 | tf_op jit(solution)/shard_map/while/body/eval_jaxpr/ppermute | solution.py:197
  77.7 6.6 %collective-permute-start.3 = (f32[160,128]{1,0:T(8,128)S(1)}, f32[160,128]{1,0:T(8,128)S(1)}, u32[]{:S(2)}, u32[]{:S(2)}) collective-permute-start(f32[160,128]{1,0:T(8,128)S(1)} %four.3.kept_ref), channel_id=1, source_target_pairs={{0,6},{1,7},{2,4},{3,5},{4,2},{5,3},{6,0},{7,1},{8,14},{9,15},{10,... | collective-permute-start | bytes 245768 | tf_op jit(solution)/shard_map/while/body/eval_jaxpr/ppermute | solution.py:197
  84.3 4.5 %collective-permute-start.8 = (f32[160,128]{1,0:T(8,128)S(1)}, f32[160,128]{1,0:T(8,128)S(1)}, u32[]{:S(2)}, u32[]{:S(2)}) collective-permute-start(f32[160,128]{1,0:T(8,128)S(1)} %get-tuple-element.291.kept_ref), channel_id=1, source_target_pairs={{0,8},{1,9},{2,10},{3,11},{4,12},{5,13},{6,14},{7,15},{8,0},{9,1},... | collective-permute-start | bytes 245768 | tf_op jit(solution)/shard_map/while/body/eval_jaxpr/ppermute | solution.py:197
  88.9 5.6 %collective-permute-start.9 = (f32[128,128]{1,0:T(8,128)S(1)}, f32[128,128]{1,0:T(8,128)S(1)}, u32[]{:S(2)}, u32[]{:S(2)}) collective-permute-start(f32[128,128]{1,0:T(8,128)S(1)} %add.17.kept_ref), channel_id=1, source_target_pairs={{0,24},{1,25},{2,26},{3,27},{4,28},{5,29},{6,30},{7,31},{8,16},{9,... | collective-permute-start | bytes 196616 | tf_op jit(solution)/shard_map/while/body/eval_jaxpr/ppermute | solution.py:197
  89.4 13.4 %collective-permute-start.4 = (f32[160,128]{1,0:T(8,128)S(1)}, f32[160,128]{1,0:T(8,128)S(1)}, u32[]{:S(2)}, u32[]{:S(2)}) collective-permute-start(f32[160,128]{1,0:T(8,128)S(1)} %get-tuple-element.286), channel_id=1, source_target_pairs={{0,1},{1,0},{2,3},{3,2},{4,5},{5,4},{6,7},{7,6},{8,9},{9,8},{10,11... | collective-permute-start | bytes 245768 | tf_op jit(solution)/shard_map/while/body/eval_jaxpr/ppermute | solution.py:197
  94.4 4.4 %collective-permute-start.10 = (f32[96,128]{1,0:T(8,128)S(1)}, f32[96,128]{1,0:T(8,128)S(1)}, u32[]{:S(2)}, u32[]{:S(2)}) collective-permute-start(f32[96,128]{1,0:T(8,128)S(1)} %add.18.kept_ref), channel_id=1, source_target_pairs={{0,32},{32,0},{64,96},{96,64},{128,160},{160,128},{192,224},{224,1... | collective-permute-start | bytes 147464 | tf_op jit(solution)/shard_map/while/body/eval_jaxpr/ppermute | solution.py:197
  94.5 5.4 %collective-permute-start.5 = (f32[96,128]{1,0:T(8,128)S(1)}, f32[96,128]{1,0:T(8,128)S(1)}, u32[]{:S(2)}, u32[]{:S(2)}) collective-permute-start(f32[96,128]{1,0:T(8,128)S(1)} %get-tuple-element.287), channel_id=1, source_target_pairs={{0,2},{1,3},{2,0},{3,1},{4,6},{5,7},{6,4},{7,5},{8,10},{9,11},{10,... | collective-permute-start | bytes 147464 | tf_op jit(solution)/shard_map/while/body/eval_jaxpr/ppermute | solution.py:197
  96.9 5.9 %collective-permute-start.6 = (f32[96,128]{1,0:T(8,128)S(1)}, f32[96,128]{1,0:T(8,128)S(1)}, u32[]{:S(2)}, u32[]{:S(2)}) collective-permute-start(f32[96,128]{1,0:T(8,128)S(1)} %get-tuple-element.288), channel_id=1, source_target_pairs={{0,3},{1,2},{2,1},{3,0},{4,7},{5,6},{6,5},{7,4},{8,11},{9,10},{10,... | collective-permute-start | bytes 147464 | tf_op jit(solution)/shard_map/while/body/eval_jaxpr/ppermute | solution.py:197
  98.9 5.1 %collective-permute-start.11 = (f32[64,128]{1,0:T(8,128)S(1)}, f32[64,128]{1,0:T(8,128)S(1)}, u32[]{:S(2)}, u32[]{:S(2)}) collective-permute-start(f32[64,128]{1,0:T(8,128)S(1)} %add.19.kept_ref), channel_id=1, source_target_pairs={{0,64},{32,96},{64,0},{96,32},{128,192},{160,224},{192,128},{224,1... | collective-permute-start | bytes 98312 | tf_op jit(solution)/shard_map/while/body/eval_jaxpr/ppermute | solution.py:197
  102.8 5.9 %collective-permute-start.7 = (f32[32,128]{1,0:T(8,128)S(1)}, f32[32,128]{1,0:T(8,128)S(1)}, u32[]{:S(2)}, u32[]{:S(2)}) collective-permute-start(f32[32,128]{1,0:T(8,128)S(1)} %get-tuple-element.290.refs_0_), channel_id=1, source_target_pairs={{0,6},{1,7},{2,4},{3,5},{4,2},{5,3},{6,0},{7,1},{8,14},{9,15},{10,... | collective-permute-start | bytes 49160 | tf_op jit(solution)/shard_map/while/body/eval_jaxpr/ppermute | solution.py:197
  104.0 5.0 %collective-permute-start.12 = (f32[32,128]{1,0:T(8,128)S(1)}, f32[32,128]{1,0:T(8,128)S(1)}, u32[]{:S(2)}, u32[]{:S(2)}) collective-permute-start(f32[32,128]{1,0:T(8,128)S(1)} %add.20), channel_id=1, source_target_pairs={{0,192},{32,224},{64,128},{96,160},{128,64},{160,96},{192,0},{224,... | collective-permute-start | bytes 49160 | tf_op jit(solution)/shard_map/while/body/eval_jaxpr/ppermute | solution.py:197
  109.0 10.8 %collective-permute-start.13 = (f32[256,128]{1,0:T(8,128)S(1)}, f32[256,128]{1,0:T(8,128)S(1)}, u32[]{:S(2)}, u32[]{:S(2)}) collective-permute-start(f32[256,128]{1,0:T(8,128)S(1)} %get-tuple-element.292.own), channel_id=1, source_target_pairs={{0,1},{1,0},{2,3},{3,2},{4,5},{5,4},{6,7},{7,6},{8,9},{9,8},{10,11... | collective-permute-start | bytes 393224 | tf_op jit(solution)/shard_map/while/body/eval_jaxpr/ppermute | solution.py:197
  110.5 6.7 %collective-permute-start.15 = (f32[192,128]{1,0:T(8,128)S(1)}, f32[192,128]{1,0:T(8,128)S(1)}, u32[]{:S(2)}, u32[]{:S(2)}) collective-permute-start(f32[192,128]{1,0:T(8,128)S(1)} %get-tuple-element.293), channel_id=1, source_target_pairs={{0,3},{1,2},{2,1},{3,0},{4,7},{5,6},{6,5},{7,4},{8,11},{9,10},{10,... | collective-permute-start | bytes 294920 | tf_op jit(solution)/shard_map/while/body/eval_jaxpr/ppermute | solution.py:197
  112.5 7.4 %collective-permute-start.14 = (f32[192,128]{1,0:T(8,128)S(1)}, f32[192,128]{1,0:T(8,128)S(1)}, u32[]{:S(2)}, u32[]{:S(2)}) collective-permute-start(f32[192,128]{1,0:T(8,128)S(1)} %get-tuple-element.293), channel_id=1, source_target_pairs={{0,2},{1,3},{2,0},{3,1},{4,6},{5,7},{6,4},{7,5},{8,10},{9,11},{10,... | collective-permute-start | bytes 294920 | tf_op jit(solution)/shard_map/while/body/eval_jaxpr/ppermute | solution.py:197
  126.0 7.3 %collective-permute-start.2 = (f32[160,128]{1,0:T(8,128)}, f32[160,128]{1,0:T(8,128)S(1)}, u32[]{:S(2)}, u32[]{:S(2)}) collective-permute-start(f32[160,128]{1,0:T(8,128)} %get-tuple-element.323), channel_id=1, source_target_pairs={{0,3},{1,2},{2,1},{3,0},{4,7},{5,6},{6,5},{7,4},{8,11},{9,10},{10,... | collective-permute-start | bytes 245768 | tf_op jit(solution)/shard_map/while/body/eval_jaxpr/ppermute | solution.py:197
  128.2 6.7 %collective-permute-start.1 = (f32[160,128]{1,0:T(8,128)}, f32[160,128]{1,0:T(8,128)S(1)}, u32[]{:S(2)}, u32[]{:S(2)}) collective-permute-start(f32[160,128]{1,0:T(8,128)} %get-tuple-element.322), channel_id=1, source_target_pairs={{0,2},{1,3},{2,0},{3,1},{4,6},{5,7},{6,4},{7,5},{8,10},{9,11},{10,... | collective-permute-start | bytes 245768 | tf_op jit(solution)/shard_map/while/body/eval_jaxpr/ppermute | solution.py:197
  128.2 6.7 %collective-permute-start = (f32[160,128]{1,0:T(8,128)}, f32[160,128]{1,0:T(8,128)S(1)}, u32[]{:S(2)}, u32[]{:S(2)}) collective-permute-start(f32[160,128]{1,0:T(8,128)} %get-tuple-element.321), channel_id=1, source_target_pairs={{0,1},{1,0},{2,3},{3,2},{4,5},{5,4},{6,7},{7,6},{8,9},{9,8},{10,11... | collective-permute-start | bytes 245768 | tf_op jit(solution)/shard_map/while/body/eval_jaxpr/ppermute | solution.py:197
  134.9 6.6 %collective-permute-start.3 = (f32[160,128]{1,0:T(8,128)S(1)}, f32[160,128]{1,0:T(8,128)S(1)}, u32[]{:S(2)}, u32[]{:S(2)}) collective-permute-start(f32[160,128]{1,0:T(8,128)S(1)} %four.3.kept_ref), channel_id=1, source_target_pairs={{0,6},{1,7},{2,4},{3,5},{4,2},{5,3},{6,0},{7,1},{8,14},{9,15},{10,... | collective-permute-start | bytes 245768 | tf_op jit(solution)/shard_map/while/body/eval_jaxpr/ppermute | solution.py:197
  141.6 4.5 %collective-permute-start.8 = (f32[160,128]{1,0:T(8,128)S(1)}, f32[160,128]{1,0:T(8,128)S(1)}, u32[]{:S(2)}, u32[]{:S(2)}) collective-permute-start(f32[160,128]{1,0:T(8,128)S(1)} %get-tuple-element.291.kept_ref), channel_id=1, source_target_pairs={{0,8},{1,9},{2,10},{3,11},{4,12},{5,13},{6,14},{7,15},{8,0},{9,1},... | collective-permute-start | bytes 245768 | tf_op jit(solution)/shard_map/while/body/eval_jaxpr/ppermute | solution.py:197
  146.1 5.6 %collective-permute-start.9 = (f32[128,128]{1,0:T(8,128)S(1)}, f32[128,128]{1,0:T(8,128)S(1)}, u32[]{:S(2)}, u32[]{:S(2)}) collective-permute-start(f32[128,128]{1,0:T(8,128)S(1)} %add.17.kept_ref), channel_id=1, source_target_pairs={{0,24},{1,25},{2,26},{3,27},{4,28},{5,29},{6,30},{7,31},{8,16},{9,... | collective-permute-start | bytes 196616 | tf_op jit(solution)/shard_map/while/body/eval_jaxpr/ppermute | solution.py:197
  146.7 13.5 %collective-permute-start.4 = (f32[160,128]{1,0:T(8,128)S(1)}, f32[160,128]{1,0:T(8,128)S(1)}, u32[]{:S(2)}, u32[]{:S(2)}) collective-permute-start(f32[160,128]{1,0:T(8,128)S(1)} %get-tuple-element.286), channel_id=1, source_target_pairs={{0,1},{1,0},{2,3},{3,2},{4,5},{5,4},{6,7},{7,6},{8,9},{9,8},{10,11... | collective-permute-start | bytes 245768 | tf_op jit(solution)/shard_map/while/body/eval_jaxpr/ppermute | solution.py:197
  151.7 2.7 %collective-permute-start.10 = (f32[96,128]{1,0:T(8,128)S(1)}, f32[96,128]{1,0:T(8,128)S(1)}, u32[]{:S(2)}, u32[]{:S(2)}) collective-permute-start(f32[96,128]{1,0:T(8,128)S(1)} %add.18.kept_ref), channel_id=1, source_target_pairs={{0,32},{32,0},{64,96},{96,64},{128,160},{160,128},{192,224},{224,1... | collective-permute-start | bytes 147464 | tf_op jit(solution)/shard_map/while/body/eval_jaxpr/ppermute | solution.py:197
  151.8 5.8 %collective-permute-start.5 = (f32[96,128]{1,0:T(8,128)S(1)}, f32[96,128]{1,0:T(8,128)S(1)}, u32[]{:S(2)}, u32[]{:S(2)}) collective-permute-start(f32[96,128]{1,0:T(8,128)S(1)} %get-tuple-element.287), channel_id=1, source_target_pairs={{0,2},{1,3},{2,0},{3,1},{4,6},{5,7},{6,4},{7,5},{8,10},{9,11},{10,... | collective-permute-start | bytes 147464 | tf_op jit(solution)/shard_map/while/body/eval_jaxpr/ppermute | solution.py:197
  154.3 5.9 %collective-permute-start.6 = (f32[96,128]{1,0:T(8,128)S(1)}, f32[96,128]{1,0:T(8,128)S(1)}, u32[]{:S(2)}, u32[]{:S(2)}) collective-permute-start(f32[96,128]{1,0:T(8,128)S(1)} %get-tuple-element.288), channel_id=1, source_target_pairs={{0,3},{1,2},{2,1},{3,0},{4,7},{5,6},{6,5},{7,4},{8,11},{9,10},{10,... | collective-permute-start | bytes 147464 | tf_op jit(solution)/shard_map/while/body/eval_jaxpr/ppermute | solution.py:197
  154.4 8.0 %collective-permute-start.11 = (f32[64,128]{1,0:T(8,128)S(1)}, f32[64,128]{1,0:T(8,128)S(1)}, u32[]{:S(2)}, u32[]{:S(2)}) collective-permute-start(f32[64,128]{1,0:T(8,128)S(1)} %add.19.kept_ref), channel_id=1, source_target_pairs={{0,64},{32,96},{64,0},{96,32},{128,192},{160,224},{192,128},{224,1... | collective-permute-start | bytes 98312 | tf_op jit(solution)/shard_map/while/body/eval_jaxpr/ppermute | solution.py:197
  160.2 5.9 %collective-permute-start.7 = (f32[32,128]{1,0:T(8,128)S(1)}, f32[32,128]{1,0:T(8,128)S(1)}, u32[]{:S(2)}, u32[]{:S(2)}) collective-permute-start(f32[32,128]{1,0:T(8,128)S(1)} %get-tuple-element.290.refs_0_), channel_id=1, source_target_pairs={{0,6},{1,7},{2,4},{3,5},{4,2},{5,3},{6,0},{7,1},{8,14},{9,15},{10,... | collective-permute-start | bytes 49160 | tf_op jit(solution)/shard_map/while/body/eval_jaxpr/ppermute | solution.py:197
  162.4 5.0 %collective-permute-start.12 = (f32[32,128]{1,0:T(8,128)S(1)}, f32[32,128]{1,0:T(8,128)S(1)}, u32[]{:S(2)}, u32[]{:S(2)}) collective-permute-start(f32[32,128]{1,0:T(8,128)S(1)} %add.20), channel_id=1, source_target_pairs={{0,192},{32,224},{64,128},{96,160},{128,64},{160,96},{192,0},{224,... | collective-permute-start | bytes 49160 | tf_op jit(solution)/shard_map/while/body/eval_jaxpr/ppermute | solution.py:197
  167.4 10.7 %collective-permute-start.13 = (f32[256,128]{1,0:T(8,128)S(1)}, f32[256,128]{1,0:T(8,128)S(1)}, u32[]{:S(2)}, u32[]{:S(2)}) collective-permute-start(f32[256,128]{1,0:T(8,128)S(1)} %get-tuple-element.292.own), channel_id=1, source_target_pairs={{0,1},{1,0},{2,3},{3,2},{4,5},{5,4},{6,7},{7,6},{8,9},{9,8},{10,11... | collective-permute-start | bytes 393224 | tf_op jit(solution)/shard_map/while/body/eval_jaxpr/ppermute | solution.py:197
  168.8 6.6 %collective-permute-start.15 = (f32[192,128]{1,0:T(8,128)S(1)}, f32[192,128]{1,0:T(8,128)S(1)}, u32[]{:S(2)}, u32[]{:S(2)}) collective-permute-start(f32[192,128]{1,0:T(8,128)S(1)} %get-tuple-element.293), channel_id=1, source_target_pairs={{0,3},{1,2},{2,1},{3,0},{4,7},{5,6},{6,5},{7,4},{8,11},{9,10},{10,... | collective-permute-start | bytes 294920 | tf_op jit(solution)/shard_map/while/body/eval_jaxpr/ppermute | solution.py:197
  170.7 7.4 %collective-permute-start.14 = (f32[192,128]{1,0:T(8,128)S(1)}, f32[192,128]{1,0:T(8,128)S(1)}, u32[]{:S(2)}, u32[]{:S(2)}) collective-permute-start(f32[192,128]{1,0:T(8,128)S(1)} %get-tuple-element.293), channel_id=1, source_target_pairs={{0,2},{1,3},{2,0},{3,1},{4,6},{5,7},{6,4},{7,5},{8,10},{9,11},{10,... | collective-permute-start | bytes 294920 | tf_op jit(solution)/shard_map/while/body/eval_jaxpr/ppermute | solution.py:197
  184.3 4.7 %collective-permute-start.16 = (f32[160,128]{1,0:T(8,128)}, f32[160,128]{1,0:T(8,128)S(1)}, u32[]{:S(2)}, u32[]{:S(2)}) collective-permute-start(f32[160,128]{1,0:T(8,128)} %get-tuple-element.132), channel_id=1, source_target_pairs={{0,1},{1,0},{2,3},{3,2},{4,5},{5,4},{6,7},{7,6},{8,9},{9,8},{10,11... | collective-permute-start | bytes 245768 | tf_op jit(solution)/shard_map/ppermute | solution.py:197
  184.3 7.8 %collective-permute-start.17 = (f32[160,128]{1,0:T(8,128)}, f32[160,128]{1,0:T(8,128)S(1)}, u32[]{:S(2)}, u32[]{:S(2)}) collective-permute-start(f32[160,128]{1,0:T(8,128)} %get-tuple-element.133), channel_id=1, source_target_pairs={{0,2},{1,3},{2,0},{3,1},{4,6},{5,7},{6,4},{7,5},{8,10},{9,11},{10,... | collective-permute-start | bytes 245768 | tf_op jit(solution)/shard_map/ppermute | solution.py:197
  187.0 6.6 %collective-permute-start.18 = (f32[160,128]{1,0:T(8,128)}, f32[160,128]{1,0:T(8,128)S(1)}, u32[]{:S(2)}, u32[]{:S(2)}) collective-permute-start(f32[160,128]{1,0:T(8,128)} %get-tuple-element.134), channel_id=1, source_target_pairs={{0,3},{1,2},{2,1},{3,0},{4,7},{5,6},{6,5},{7,4},{8,11},{9,10},{10,... | collective-permute-start | bytes 245768 | tf_op jit(solution)/shard_map/ppermute | solution.py:197
  193.6 6.9 %collective-permute-start.19 = (f32[160,128]{1,0:T(8,128)S(1)}, f32[160,128]{1,0:T(8,128)S(1)}, u32[]{:S(2)}, u32[]{:S(2)}) collective-permute-start(f32[160,128]{1,0:T(8,128)S(1)} %four.2.kept_ref), channel_id=1, source_target_pairs={{0,6},{1,7},{2,4},{3,5},{4,2},{5,3},{6,0},{7,1},{8,14},{9,15},{10,... | collective-permute-start | bytes 245768 | tf_op jit(solution)/shard_map/ppermute | solution.py:197
  200.5 4.5 %collective-permute-start.24 = (f32[160,128]{1,0:T(8,128)S(1)}, f32[160,128]{1,0:T(8,128)S(1)}, u32[]{:S(2)}, u32[]{:S(2)}) collective-permute-start(f32[160,128]{1,0:T(8,128)S(1)} %get-tuple-element.144.kept_ref), channel_id=1, source_target_pairs={{0,8},{1,9},{2,10},{3,11},{4,12},{5,13},{6,14},{7,15},{8,0},{9,1},... | collective-permute-start | bytes 245768 | tf_op jit(solution)/shard_map/ppermute | solution.py:197
  205.0 5.6 %collective-permute-start.25 = (f32[128,128]{1,0:T(8,128)S(1)}, f32[128,128]{1,0:T(8,128)S(1)}, u32[]{:S(2)}, u32[]{:S(2)}) collective-permute-start(f32[128,128]{1,0:T(8,128)S(1)} %add.13.kept_ref), channel_id=1, source_target_pairs={{0,24},{1,25},{2,26},{3,27},{4,28},{5,29},{6,30},{7,31},{8,16},{9,... | collective-permute-start | bytes 196616 | tf_op jit(solution)/shard_map/ppermute | solution.py:197
  205.6 13.3 %collective-permute-start.20 = (f32[160,128]{1,0:T(8,128)S(1)}, f32[160,128]{1,0:T(8,128)S(1)}, u32[]{:S(2)}, u32[]{:S(2)}) collective-permute-start(f32[160,128]{1,0:T(8,128)S(1)} %get-tuple-element.138), channel_id=1, source_target_pairs={{0,1},{1,0},{2,3},{3,2},{4,5},{5,4},{6,7},{7,6},{8,9},{9,8},{10,11... | collective-permute-start | bytes 245768 | tf_op jit(solution)/shard_map/ppermute | solution.py:197
  210.6 4.2 %collective-permute-start.26 = (f32[96,128]{1,0:T(8,128)S(1)}, f32[96,128]{1,0:T(8,128)S(1)}, u32[]{:S(2)}, u32[]{:S(2)}) collective-permute-start(f32[96,128]{1,0:T(8,128)S(1)} %add.14.kept_ref), channel_id=1, source_target_pairs={{0,32},{32,0},{64,96},{96,64},{128,160},{160,128},{192,224},{224,1... | collective-permute-start | bytes 147464 | tf_op jit(solution)/shard_map/ppermute | solution.py:197
  210.7 6.6 %collective-permute-start.21 = (f32[96,128]{1,0:T(8,128)S(1)}, f32[96,128]{1,0:T(8,128)S(1)}, u32[]{:S(2)}, u32[]{:S(2)}) collective-permute-start(f32[96,128]{1,0:T(8,128)S(1)} %get-tuple-element.140), channel_id=1, source_target_pairs={{0,2},{1,3},{2,0},{3,1},{4,6},{5,7},{6,4},{7,5},{8,10},{9,11},{10,... | collective-permute-start | bytes 147464 | tf_op jit(solution)/shard_map/ppermute | solution.py:197
  213.0 5.9 %collective-permute-start.22 = (f32[96,128]{1,0:T(8,128)S(1)}, f32[96,128]{1,0:T(8,128)S(1)}, u32[]{:S(2)}, u32[]{:S(2)}) collective-permute-start(f32[96,128]{1,0:T(8,128)S(1)} %get-tuple-element.141), channel_id=1, source_target_pairs={{0,3},{1,2},{2,1},{3,0},{4,7},{5,6},{6,5},{7,4},{8,11},{9,10},{10,... | collective-permute-start | bytes 147464 | tf_op jit(solution)/shard_map/ppermute | solution.py:197
  214.8 4.6 %collective-permute-start.27 = (f32[64,128]{1,0:T(8,128)S(1)}, f32[64,128]{1,0:T(8,128)S(1)}, u32[]{:S(2)}, u32[]{:S(2)}) collective-permute-start(f32[64,128]{1,0:T(8,128)S(1)} %add.15.kept_ref), channel_id=1, source_target_pairs={{0,64},{32,96},{64,0},{96,32},{128,192},{160,224},{192,128},{224,1... | collective-permute-start | bytes 98312 | tf_op jit(solution)/shard_map/ppermute | solution.py:197
  219.0 5.9 %collective-permute-start.23 = (f32[32,128]{1,0:T(8,128)S(1)}, f32[32,128]{1,0:T(8,128)S(1)}, u32[]{:S(2)}, u32[]{:S(2)}) collective-permute-start(f32[32,128]{1,0:T(8,128)S(1)} %get-tuple-element.143.refs_0_), channel_id=1, source_target_pairs={{0,6},{1,7},{2,4},{3,5},{4,2},{5,3},{6,0},{7,1},{8,14},{9,15},{10,... | collective-permute-start | bytes 49160 | tf_op jit(solution)/shard_map/ppermute | solution.py:197
  219.3 5.5 %collective-permute-start.28 = (f32[32,128]{1,0:T(8,128)S(1)}, f32[32,128]{1,0:T(8,128)S(1)}, u32[]{:S(2)}, u32[]{:S(2)}) collective-permute-start(f32[32,128]{1,0:T(8,128)S(1)} %add.16), channel_id=1, source_target_pairs={{0,192},{32,224},{64,128},{96,160},{128,64},{160,96},{192,0},{224,... | collective-permute-start | bytes 49160 | tf_op jit(solution)/shard_map/ppermute | solution.py:197
  224.9 10.8 %collective-permute-start.29 = (f32[256,128]{1,0:T(8,128)S(1)}, f32[256,128]{1,0:T(8,128)S(1)}, u32[]{:S(2)}, u32[]{:S(2)}) collective-permute-start(f32[256,128]{1,0:T(8,128)S(1)} %get-tuple-element.145.refs_1_), channel_id=1, source_target_pairs={{0,1},{1,0},{2,3},{3,2},{4,5},{5,4},{6,7},{7,6},{8,9},{9,8},{10,11... | collective-permute-start | bytes 393224 | tf_op jit(solution)/shard_map/ppermute | solution.py:197
  226.5 6.5 %collective-permute-start.31 = (f32[192,128]{1,0:T(8,128)S(1)}, f32[192,128]{1,0:T(8,128)S(1)}, u32[]{:S(2)}, u32[]{:S(2)}) collective-permute-start(f32[192,128]{1,0:T(8,128)S(1)} %get-tuple-element.146), channel_id=1, source_target_pairs={{0,3},{1,2},{2,1},{3,0},{4,7},{5,6},{6,5},{7,4},{8,11},{9,10},{10,... | collective-permute-start | bytes 294920 | tf_op jit(solution)/shard_map/ppermute | solution.py:197
  228.4 7.3 %collective-permute-start.30 = (f32[192,128]{1,0:T(8,128)S(1)}, f32[192,128]{1,0:T(8,128)S(1)}, u32[]{:S(2)}, u32[]{:S(2)}) collective-permute-start(f32[192,128]{1,0:T(8,128)S(1)} %get-tuple-element.146), channel_id=1, source_target_pairs={{0,2},{1,3},{2,0},{3,1},{4,6},{5,7},{6,4},{7,5},{8,10},{9,11},{10,... | collective-permute-start | bytes 294920 | tf_op jit(solution)/shard_map/ppermute | solution.py:197
  (5 other events, 78.6 us)
where the time goes:
time: 239 us; the launch traced here: 238 us
  waiting for transfers between devices  104 us (44%)
  starting transfers between devices  89.5 us (37%)
  Pallas kernels  43.1 us (18%)
    ppermute x64, waiting for transfers between devices, from_partner(): return lax.ppermute(value, axis, pairs)  104 us
    ppermute x64, starting transfers between devices, from_partner(): return lax.ppermute(value, axis, pairs)  89.5 us
    pallas_call x41, Pallas kernels, call(): pl.pallas_call(kernel, out_shape=outs, in_specs=[VMEM] * len(args), out_s...  43.1 us
  transfers between devices with their start and end apart: 64, of which 41 were waited for; matrix products, arithmetic and copies ran while one was open for 0% of the time, Pallas kernels for 7%

commit v1 on v0

--- a/solution.py
+++ b/solution.py
@@ -41,7 +41,7 @@
 
 
 def project(state_ref, v_ref, outs, parts_ref):
-    sends, keep_ref, early, early_keep_ref = outs[:3], outs[3], outs[4:7], outs[7]
+    *sends, keep_ref = outs
     own_half, own_quarter = place()
     wide = state_ref.shape[0]
     half, quarter = wide // 2, wide // 4
@@ -55,16 +55,14 @@
         return 0
 
     lax.fori_loop(0, levels // 2, two_levels, 0)
-    early[0][pl.ds(0, wide), :] = parts_ref[0]
-    early[1][pl.ds(0, half), :] = parts_ref[1, section(own_half, half), :]
-    early[2][pl.ds(0, half), :] = parts_ref[1, section(1 - own_half, half), :]
-    targets = ((early[0], wide), (early[1], half), (early[2], half), (early_keep_ref, 0))
-    places = quarters_of(own_quarter)
-    for (ref, start), index in zip(targets, places):
-        ref[pl.ds(start, quarter), :] = parts_ref[2, section(index, quarter), :]
-    for level in range(3, levels):
-        for ref, index in zip((*sends, keep_ref), places):
-            ref[pl.ds((level - 3) * quarter, quarter), :] = parts_ref[level, section(index, quarter), :]
+    sends[0][pl.ds(0, wide), :] = parts_ref[0]
+    sends[1][pl.ds(0, half), :] = parts_ref[1, section(own_half, half), :]
+    sends[2][pl.ds(0, half), :] = parts_ref[1, section(1 - own_half, half), :]
+    targets = ((sends[0], wide), (sends[1], half), (sends[2], half), (keep_ref, 0))
+    for (ref, start), index in zip(targets, quarters_of(own_quarter)):
+        for level in range(2, levels):
+            rows = pl.ds(start + (level - 2) * quarter, quarter)
+            ref[rows, :] = parts_ref[level, section(index, quarter), :]
 
 
 def first_kernel(state_ref, v_ref, *refs):
@@ -136,28 +134,14 @@
     lax.fori_loop(0, dev_rows // leaf, one_leaf, 0)
 
 
-def four_kernel(keep_ref, near_ref, next_ref, far_ref, out_ref):
-    out_ref[...] = (keep_ref[...] + near_ref[...]) + (next_ref[...] + far_ref[...])
-
-
-def line_kernel(arrived_ref, kept_ref, *refs):
-    early, (out_ref, *late) = refs[:3], refs[3:]
-    out_ref[...] = kept_ref[...] + arrived_ref[...]
-    for source, target in zip(early, late):
-        target[...] = source[...]
-
-
-def early_kernel(keep_ref, near_ref, next_ref, far_ref, one_ref, two_ref):
-    half, quarter = one_ref.shape[0], two_ref.shape[0]
-    skip = near_ref.shape[0] - quarter
+def four_kernel(keep_ref, near_ref, next_ref, far_ref, one_ref, out_ref):
+    half, rows = one_ref.shape[0], out_ref.shape[0]
     one_ref[...] = next_ref[pl.ds(0, half), :] + far_ref[pl.ds(0, half), :]
-    two_ref[...] = (keep_ref[...] + near_ref[pl.ds(skip, quarter), :]) + (
-        next_ref[pl.ds(half, quarter), :] + far_ref[pl.ds(half, quarter), :]
-    )
-
-
-def add_kernel(arrived_ref, kept_ref, *refs):
-    out_ref = refs[-1]
+    rest = pl.ds(half, rows)
+    out_ref[...] = (keep_ref[...] + near_ref[pl.ds(2 * half, rows), :]) + (next_ref[rest, :] + far_ref[rest, :])
+
+
+def add_kernel(arrived_ref, kept_ref, out_ref):
     rows = out_ref.shape[0]
     out_ref[...] = (
         kept_ref[pl.ds(kept_ref.shape[0] - rows, rows), :]
@@ -198,28 +182,21 @@
 
 
 def exchange(parts):
-    sends, keep, early, early_keep = parts[:3], parts[3], parts[4:7], parts[7]
+    *sends, keep = parts
     rows, rank = keep.shape
-    quarter = early_keep.shape[0]
-    half = 2 * quarter
-    masks = (1, 2, 3)
-    arrived = [from_partner(send, "lo", mask) for send, mask in zip(sends, masks)]
-    total = call(four_kernel, "four", stack(rows, rank), keep, *arrived)
-    shapes = (stack(rows, rank), *(stack(send.shape[0], rank) for send in early))
-    total, *early = call(line_kernel, "line", shapes, from_partner(total, "lo", 6), total, *early)
-    early = [from_partner(send, "lo", mask) for send, mask in zip(early, masks)]
-    one, two = call(early_kernel, "early", (stack(half, rank), stack(quarter, rank)), early_keep, *early)
-    found = [from_partner(two, "lo", 6)]
-    for axis, mask in (("lo", 8), ("lo", 24), ("hi", 1), ("hi", 2), ("hi", 6)):
+    half = sends[1].shape[0] - rows
+    quarter = half // 2
+    arrived = [from_partner(send, "lo", mask) for send, mask in zip(sends, (1, 2, 3))]
+    one, total = call(four_kernel, "four", (stack(half, rank), stack(rows, rank)), keep, *arrived)
+    found = []
+    for axis, mask in (("lo", 6), ("lo", 8), ("lo", 24), ("hi", 1), ("hi", 2), ("hi", 6)):
         value = from_partner(total, axis, mask)
         found.append(value)
-        rows = total.shape[0] - quarter
-        if rows:
-            ahead = (two,) if (axis, mask) == ("hi", 2) else ()
-            total = call(add_kernel, "add", stack(rows, rank), value, total, *ahead)
-    rows = len(found) * quarter
+        left = total.shape[0] - quarter
+        if left:
+            total = call(add_kernel, "add", stack(left, rank), value, total)
     long, short = call(join_kernel, "join", (stack(half + rows, rank), stack(rows, rank)), one, *found)
-    return early[0], long, from_partner(long, "lo", 1), from_partner(short, "lo", 2), from_partner(short, "lo", 3)
+    return arrived[0], long, from_partner(long, "lo", 1), from_partner(short, "lo", 2), from_partner(short, "lo", 3)
 
 
 def local(vectors, leaves, u_local, v_local, u_upper, v_upper):
@@ -232,8 +209,8 @@
     scales = [1.0 / math.sqrt(leaf * 2**level * level_count) for level in range(level_count)]
     upper_scales = scales[local_count:]
     half, quarter = wide // 2, wide // 4
-    upper = (upper_count - 3) * quarter
-    rows = [upper] * 4 + [wide + quarter, half + quarter, half + quarter, quarter]
+    upper = (upper_count - 2) * quarter
+    rows = [wide + upper, half + upper, half + upper, upper]
     part_shapes = tuple(stack(number, rank) for number in rows)
     state_shape = jax.ShapeDtypeStruct((wide, dev_rows), jnp.bfloat16)
     base_shape = jax.ShapeDtypeStruct((wide, dev_rows), jnp.float32)
@@ -242,28 +219,23 @@
     local_scratch = [pltpu.VMEM((local_count, dev_rows // leaf, wide, rank), jnp.bfloat16)]
     state = vectors
     parts = call(first_kernel, "first", part_shapes, state, v_upper, scratch=part_scratch)
-
-    def found(state, parts):
+    for step in range(ITERS):
+        found = exchange(parts)
         base = call(
             functools.partial(local_kernel, scales[:local_count]), "local", base_shape, state, leaves, u_local, v_local,
             scratch=local_scratch,
         )
-        return *exchange(parts), base
-
-    def step(_, carry):
-        state, *parts = carry
-        return tuple(
-            call(
+        if step < ITERS - 1:
+            state, *parts = call(
                 functools.partial(middle_kernel, upper_scales), "middle", (state_shape, *part_shapes),
-                *found(state, parts), u_upper, v_upper, scratch=coef_scratch + part_scratch,
+                *found, base, u_upper, v_upper, scratch=coef_scratch + part_scratch,
             )
-        )
-
-    state, *parts = lax.fori_loop(0, ITERS - 1, step, (state, *parts))
-    return call(
-        functools.partial(last_kernel, upper_scales), "last", state_shape, *found(state, parts), u_upper,
-        scratch=coef_scratch,
-    )
+        else:
+            state = call(
+                functools.partial(last_kernel, upper_scales), "last", state_shape, *found, base, u_upper,
+                scratch=coef_scratch,
+            )
+    return state
 
 
 def solution(mesh):

time: 239 us -> 228 us (0.954)
  waiting for transfers between devices: 104 us -> 123 us
  Pallas kernels: 43.1 us -> 25 us
  starting transfers between devices: 89.5 us -> 72.9 us
  local copies, waits for them, and re-layouts: 1.21 us -> 6.75 us
    ppermute x64 -> x48, waiting for transfers between devices: 104 us -> 123 us  [from_partner(): return lax.ppermute(value, axis, pairs)]
    pallas_call x41 -> x37, Pallas kernels: 43.1 us -> 25 us  [call(): pl.pallas_call(kernel, out_shape=outs, in_specs=[VMEM] * len(args), out_s...]
    ppermute x64 -> x48, starting transfers between devices: 89.5 us -> 72.9 us  [from_partner(): return lax.ppermute(value, axis, pairs)]
    unnamed x5 -> x20, local copies, waits for them, and re-layouts: 1.2 us -> 6.75 us
  transfers between devices with their start and end apart: 64 -> 48, of which waited for: 41 -> 35; matrix products, arithmetic and copies ran while one was open for 0% -> 0% of each run, Pallas kernels for 7% -> 5%
where the time goes in v1:
time: 228 us
  waiting for transfers between devices  123 us (54%)
  starting transfers between devices  72.9 us (32%)
  Pallas kernels  25 us (11%)
  local copies, waits for them, and re-layouts  6.75 us (3%)
    ppermute x48, waiting for transfers between devices, from_partner(): return lax.ppermute(value, axis, pairs)  123 us
    ppermute x48, starting transfers between devices, from_partner(): return lax.ppermute(value, axis, pairs)  72.9 us
    pallas_call x37, Pallas kernels, call(): pl.pallas_call(kernel, out_shape=outs, in_specs=[VMEM] * len(args), out_s...  25 us
    unnamed x20, local copies, waits for them, and re-layouts  6.75 us
  transfers between devices with their start and end apart: 48, of which 35 were waited for; matrix products, arithmetic and copies ran while one was open for 0% of the time, Pallas kernels for 5%

profile of v1, /device:TPU:6, one launch (start us, length us, event | category | flops | bytes accessed | tf_op | source)
XLA Modules:
  0.0 228.0 jit_solution(10405552518899054322)
XLA Ops:
  0.0 2.2 copy-done
  4.5 2.0 collective-permute-start
  6.5 3.3 %collective-permute-start.1 = (f32[256,128]{1,0:T(8,128)S(1)}, f32[256,128]{1,0:T(8,128)S(1)}, u32[]{:S(2)}, u32[]{:S(2)}) collective-permute-start(f32[256,128]{1,0:T(8,128)S(1)} %get-tuple-element.42), channel_id=1, source_target_pairs={{0,2},{1,3},{2,0},{3,1},{4,6},{5,7},{6,4},{7,5},{8,10},{9,11},{10,... | collective-permute-start | bytes 393224 | tf_op jit(solution)/shard_map/ppermute | solution.py:181
  9.8 10.0 %collective-permute-done.1.next_ref = f32[256,128]{1,0:T(8,128)S(1)} collective-permute-done((f32[256,128]{1,0:T(8,128)S(1)}, f32[256,128]{1,0:T(8,128)S(1)}, u32[]{:S(2)}, u32[]{:S(2)}) %collective-permute-start.1) | collective-permute-done | bytes 131104 | tf_op jit(solution)/shard_map/ppermute | solution.py:181
  19.8 6.1 %collective-permute-start.3 = (f32[192,128]{1,0:T(8,128)S(1)}, f32[192,128]{1,0:T(8,128)S(1)}, u32[]{:S(2)}, u32[]{:S(2)}) collective-permute-start(f32[192,128]{1,0:T(8,128)S(1)} %get-tuple-element.45.kept_ref), channel_id=1, source_target_pairs={{0,6},{1,7},{2,4},{3,5},{4,2},{5,3},{6,0},{7,1},{8,14},{9,15},{10,... | collective-permute-start | bytes 294920 | tf_op jit(solution)/shard_map/ppermute | solution.py:181
  25.9 2.7 %collective-permute-done.3.arrived_ref.refs_0_ = f32[192,128]{1,0:T(8,128)S(1)} collective-permute-done((f32[192,128]{1,0:T(8,128)S(1)}, f32[192,128]{1,0:T(8,128)S(1)}, u32[]{:S(2)}, u32[]{:S(2)}) %collective-permute-start.3) | collective-permute-done | bytes 98336 | tf_op jit(solution)/shard_map/ppermute | solution.py:181
  29.6 3.6 %collective-permute-done.4.arrived_ref.refs_1_ = f32[160,128]{1,0:T(8,128)S(1)} collective-permute-done((f32[160,128]{1,0:T(8,128)S(1)}, f32[160,128]{1,0:T(8,128)S(1)}, u32[]{:S(2)}, u32[]{:S(2)}) %collective-permute-start.4) | collective-permute-done | bytes 81952 | tf_op jit(solution)/shard_map/ppermute | solution.py:181
  33.8 5.0 %collective-permute-done.5.arrived_ref.refs_2_ = f32[128,128]{1,0:T(8,128)S(1)} collective-permute-done((f32[128,128]{1,0:T(8,128)S(1)}, f32[128,128]{1,0:T(8,128)S(1)}, u32[]{:S(2)}, u32[]{:S(2)}) %collective-permute-start.5) | collective-permute-done | bytes 65568 | tf_op jit(solution)/shard_map/ppermute | solution.py:181
  40.1 1.6 collective-permute-start.7
  41.7 2.3 %collective-permute-done.7.arrived_ref.refs_4_ = f32[64,128]{1,0:T(8,128)S(1)} collective-permute-done((f32[64,128]{1,0:T(8,128)S(1)}, f32[64,128]{1,0:T(8,128)S(1)}, u32[]{:S(2)}, u32[]{:S(2)}) %collective-permute-start.7) | collective-permute-done | bytes 32800 | tf_op jit(solution)/shard_map/ppermute | solution.py:181
  44.0 3.0 %collective-permute-start.8 = (f32[32,128]{1,0:T(8,128)S(1)}, f32[32,128]{1,0:T(8,128)S(1)}, u32[]{:S(2)}, u32[]{:S(2)}) collective-permute-start(f32[32,128]{1,0:T(8,128)S(1)} %add.24), channel_id=1, source_target_pairs={{0,192},{32,224},{64,128},{96,160},{128,64},{160,96},{192,0},{224,... | collective-permute-start | bytes 49160 | tf_op jit(solution)/shard_map/ppermute | solution.py:181
  47.0 1.9 collective-permute-done.8.refs_5_
  49.0 1.3 collective-permute-start.9
  50.3 2.7 %collective-permute-start.11 = (f32[192,128]{1,0:T(8,128)S(1)}, f32[192,128]{1,0:T(8,128)S(1)}, u32[]{:S(2)}, u32[]{:S(2)}) collective-permute-start(f32[192,128]{1,0:T(8,128)S(1)} %get-tuple-element.47), channel_id=1, source_target_pairs={{0,3},{1,2},{2,1},{3,0},{4,7},{5,6},{6,5},{7,4},{8,11},{9,10},{10,... | collective-permute-start | bytes 294920 | tf_op jit(solution)/shard_map/ppermute | solution.py:181
  56.5 2.7 %local.4.base = f32[128,2048]{1,0:T(8,128)S(1)} custom-call(bf16[128,2048]{1,0:T(8,128)(2,1)S(1)} %copy-done.9, bf16[2048,512]{1,0:T(8,128)(2,1)S(1)} %copy-done.3, bf16[2,2048,128]{2,1,0:T(8,128)(2,1)S(1)} %copy-done.4, bf16[2,2048,128]{2,1,0:T(8,128)(2,1)S(1)} %copy-done.6), custom_call_target="tpu_custom_call" | custom-call | tf_op jit(solution)/shard_map/local/pallas_call | solution.py:164
  60.3 3.3 %middle.3 = (bf16[128,2048]{1,0:T(8,128)(2,1)S(1)}, f32[320,128]{1,0:T(8,128)S(1)}, f32[256,128]{1,0:T(8,128)S(1)}, f32[256,128]{1,0:T(8,128)S(1)}, f32[192,128]{1,0:T(8,128)S(1)}) custom-call(f32[320,128]{1,0:T(8,128)S(1)} %collective-permute-done.near_ref.zero, f32[256,128]{1,0:T(8,128)S(1)} %get-tuple-element.46.own, ...), custom_call_target="tpu_custom_call" | custom-call | tf_op jit(solution)/shard_map/middle/pallas_call | solution.py:164
  64.4 2.0 collective-permute-start.13
  66.4 1.7 collective-permute-start.14
  68.1 7.8 %collective-permute-done.13.next_ref = f32[256,128]{1,0:T(8,128)S(1)} collective-permute-done((f32[256,128]{1,0:T(8,128)S(1)}, f32[256,128]{1,0:T(8,128)S(1)}, u32[]{:S(2)}, u32[]{:S(2)}) %collective-permute-start.13) | collective-permute-done | bytes 131104 | tf_op jit(solution)/shard_map/ppermute | solution.py:181
  75.9 4.8 %collective-permute-start.15 = (f32[192,128]{1,0:T(8,128)S(1)}, f32[192,128]{1,0:T(8,128)S(1)}, u32[]{:S(2)}, u32[]{:S(2)}) collective-permute-start(f32[192,128]{1,0:T(8,128)S(1)} %get-tuple-element.53.kept_ref), channel_id=1, source_target_pairs={{0,6},{1,7},{2,4},{3,5},{4,2},{5,3},{6,0},{7,1},{8,14},{9,15},{10,... | collective-permute-start | bytes 294920 | tf_op jit(solution)/shard_map/ppermute | solution.py:181
  80.8 2.7 %collective-permute-done.15.arrived_ref.refs_0_ = f32[192,128]{1,0:T(8,128)S(1)} collective-permute-done((f32[192,128]{1,0:T(8,128)S(1)}, f32[192,128]{1,0:T(8,128)S(1)}, u32[]{:S(2)}, u32[]{:S(2)}) %collective-permute-start.15) | collective-permute-done | bytes 98336 | tf_op jit(solution)/shard_map/ppermute | solution.py:181
  83.6 4.4 %collective-permute-done.16.arrived_ref.refs_1_ = f32[160,128]{1,0:T(8,128)S(1)} collective-permute-done((f32[160,128]{1,0:T(8,128)S(1)}, f32[160,128]{1,0:T(8,128)S(1)}, u32[]{:S(2)}, u32[]{:S(2)}) %collective-permute-start.16) | collective-permute-done | bytes 81952 | tf_op jit(solution)/shard_map/ppermute | solution.py:181
  88.6 5.0 %collective-permute-done.17.arrived_ref.refs_2_ = f32[128,128]{1,0:T(8,128)S(1)} collective-permute-done((f32[128,128]{1,0:T(8,128)S(1)}, f32[128,128]{1,0:T(8,128)S(1)}, u32[]{:S(2)}, u32[]{:S(2)}) %collective-permute-start.17) | collective-permute-done | bytes 65568 | tf_op jit(solution)/shard_map/ppermute | solution.py:181
  95.2 3.6 %collective-permute-done.19.arrived_ref.refs_4_ = f32[64,128]{1,0:T(8,128)S(1)} collective-permute-done((f32[64,128]{1,0:T(8,128)S(1)}, f32[64,128]{1,0:T(8,128)S(1)}, u32[]{:S(2)}, u32[]{:S(2)}) %collective-permute-start.19) | collective-permute-done | bytes 32800 | tf_op jit(solution)/shard_map/ppermute | solution.py:181
  98.8 2.9 %collective-permute-start.20 = (f32[32,128]{1,0:T(8,128)S(1)}, f32[32,128]{1,0:T(8,128)S(1)}, u32[]{:S(2)}, u32[]{:S(2)}) collective-permute-start(f32[32,128]{1,0:T(8,128)S(1)} %add.29), channel_id=1, source_target_pairs={{0,192},{32,224},{64,128},{96,160},{128,64},{160,96},{192,0},{224,... | collective-permute-start | bytes 49160 | tf_op jit(solution)/shard_map/ppermute | solution.py:181
  101.8 2.0 collective-permute-done.20.refs_5_
  103.8 2.4 %collective-permute-start.21 = (f32[256,128]{1,0:T(8,128)S(1)}, f32[256,128]{1,0:T(8,128)S(1)}, u32[]{:S(2)}, u32[]{:S(2)}) collective-permute-start(f32[256,128]{1,0:T(8,128)S(1)} %get-tuple-element.54.own), channel_id=1, source_target_pairs={{0,1},{1,0},{2,3},{3,2},{4,5},{5,4},{6,7},{7,6},{8,9},{9,8},{10,11... | collective-permute-start | bytes 393224 | tf_op jit(solution)/shard_map/ppermute | solution.py:181
  106.2 2.0 collective-permute-start.23
  108.2 2.7 %local.5.base = f32[128,2048]{1,0:T(8,128)S(1)} custom-call(bf16[128,2048]{1,0:T(8,128)(2,1)S(1)} %get-tuple-element.56.state_ref, bf16[2048,512]{1,0:T(8,128)(2,1)S(1)} %copy-done.3, bf16[2,2048,128]{2,1,0:T(8,128)(2,1)S(1)} %copy-done.5, bf16[2,2048,128]{2,1,0:T(8,128)(2,1)S(1)} %copy-done.7), custom_call_target="tpu_custom_call" | custom-call | tf_op jit(solution)/shard_map/local/pallas_call | solution.py:164
  110.9 1.9 collective-permute-done.23.far
  112.8 2.8 %collective-permute-done.22.next_ = f32[192,128]{1,0:T(8,128)S(1)} collective-permute-done((f32[192,128]{1,0:T(8,128)S(1)}, f32[192,128]{1,0:T(8,128)S(1)}, u32[]{:S(2)}, u32[]{:S(2)}) %collective-permute-start.22) | collective-permute-done | bytes 98336 | tf_op jit(solution)/shard_map/ppermute | solution.py:181
  115.6 3.3 %middle.4 = (bf16[128,2048]{1,0:T(8,128)(2,1)S(1)}, f32[320,128]{1,0:T(8,128)S(1)}, f32[256,128]{1,0:T(8,128)S(1)}, f32[256,128]{1,0:T(8,128)S(1)}, f32[192,128]{1,0:T(8,128)S(1)}) custom-call(f32[320,128]{1,0:T(8,128)S(1)} %collective-permute-done.12.near_ref.zero, f32[256,128]{1,0:T(8,128)S(1)} %get-tuple-element.54.own, ...), custom_call_target="tpu_custom_call" | custom-call | tf_op jit(solution)/shard_map/middle/pallas_call | solution.py:164
  118.9 2.6 %collective-permute-start.25 = (f32[256,128]{1,0:T(8,128)S(1)}, f32[256,128]{1,0:T(8,128)S(1)}, u32[]{:S(2)}, u32[]{:S(2)}) collective-permute-start(f32[256,128]{1,0:T(8,128)S(1)} %get-tuple-element.59), channel_id=1, source_target_pairs={{0,2},{1,3},{2,0},{3,1},{4,6},{5,7},{6,4},{7,5},{8,10},{9,11},{10,... | collective-permute-start | bytes 393224 | tf_op jit(solution)/shard_map/ppermute | solution.py:181
  121.5 1.8 collective-permute-start.26
  123.3 7.8 %collective-permute-done.25.next_ref = f32[256,128]{1,0:T(8,128)S(1)} collective-permute-done((f32[256,128]{1,0:T(8,128)S(1)}, f32[256,128]{1,0:T(8,128)S(1)}, u32[]{:S(2)}, u32[]{:S(2)}) %collective-permute-start.25) | collective-permute-done | bytes 131104 | tf_op jit(solution)/shard_map/ppermute | solution.py:181
  131.2 4.3 %collective-permute-start.27 = (f32[192,128]{1,0:T(8,128)S(1)}, f32[192,128]{1,0:T(8,128)S(1)}, u32[]{:S(2)}, u32[]{:S(2)}) collective-permute-start(f32[192,128]{1,0:T(8,128)S(1)} %get-tuple-element.62.kept_ref), channel_id=1, source_target_pairs={{0,6},{1,7},{2,4},{3,5},{4,2},{5,3},{6,0},{7,1},{8,14},{9,15},{10,... | collective-permute-start | bytes 294920 | tf_op jit(solution)/shard_map/ppermute | solution.py:181
  135.5 2.7 %collective-permute-done.27.arrived_ref.refs_0_ = f32[192,128]{1,0:T(8,128)S(1)} collective-permute-done((f32[192,128]{1,0:T(8,128)S(1)}, f32[192,128]{1,0:T(8,128)S(1)}, u32[]{:S(2)}, u32[]{:S(2)}) %collective-permute-start.27) | collective-permute-done | bytes 98336 | tf_op jit(solution)/shard_map/ppermute | solution.py:181
  138.3 4.4 %collective-permute-done.28.arrived_ref.refs_1_ = f32[160,128]{1,0:T(8,128)S(1)} collective-permute-done((f32[160,128]{1,0:T(8,128)S(1)}, f32[160,128]{1,0:T(8,128)S(1)}, u32[]{:S(2)}, u32[]{:S(2)}) %collective-permute-start.28) | collective-permute-done | bytes 81952 | tf_op jit(solution)/shard_map/ppermute | solution.py:181
  143.4 5.0 %collective-permute-done.29.arrived_ref.refs_2_ = f32[128,128]{1,0:T(8,128)S(1)} collective-permute-done((f32[128,128]{1,0:T(8,128)S(1)}, f32[128,128]{1,0:T(8,128)S(1)}, u32[]{:S(2)}, u32[]{:S(2)}) %collective-permute-start.29) | collective-permute-done | bytes 65568 | tf_op jit(solution)/shard_map/ppermute | solution.py:181
  149.7 3.9 %collective-permute-done.31.arrived_ref.refs_4_ = f32[64,128]{1,0:T(8,128)S(1)} collective-permute-done((f32[64,128]{1,0:T(8,128)S(1)}, f32[64,128]{1,0:T(8,128)S(1)}, u32[]{:S(2)}, u32[]{:S(2)}) %collective-permute-start.31) | collective-permute-done | bytes 32800 | tf_op jit(solution)/shard_map/ppermute | solution.py:181
  153.6 2.9 %collective-permute-start.32 = (f32[32,128]{1,0:T(8,128)S(1)}, f32[32,128]{1,0:T(8,128)S(1)}, u32[]{:S(2)}, u32[]{:S(2)}) collective-permute-start(f32[32,128]{1,0:T(8,128)S(1)} %add.34), channel_id=1, source_target_pairs={{0,192},{32,224},{64,128},{96,160},{128,64},{160,96},{192,0},{224,... | collective-permute-start | bytes 49160 | tf_op jit(solution)/shard_map/ppermute | solution.py:181
  156.5 2.0 collective-permute-done.32.refs_5_
  158.6 2.5 %collective-permute-start.33 = (f32[256,128]{1,0:T(8,128)S(1)}, f32[256,128]{1,0:T(8,128)S(1)}, u32[]{:S(2)}, u32[]{:S(2)}) collective-permute-start(f32[256,128]{1,0:T(8,128)S(1)} %get-tuple-element.63.own), channel_id=1, source_target_pairs={{0,1},{1,0},{2,3},{3,2},{4,5},{5,4},{6,7},{7,6},{8,9},{9,8},{10,11... | collective-permute-start | bytes 393224 | tf_op jit(solution)/shard_map/ppermute | solution.py:181
  161.0 1.9 collective-permute-start.35
  163.0 2.7 %local.6.base = f32[128,2048]{1,0:T(8,128)S(1)} custom-call(bf16[128,2048]{1,0:T(8,128)(2,1)S(1)} %get-tuple-element.65.state_ref, bf16[2048,512]{1,0:T(8,128)(2,1)S(1)} %copy-done.3, bf16[2,2048,128]{2,1,0:T(8,128)(2,1)S(1)} %copy-done.5, bf16[2,2048,128]{2,1,0:T(8,128)(2,1)S(1)} %copy-done.7), custom_call_target="tpu_custom_call" | custom-call | tf_op jit(solution)/shard_map/local/pallas_call | solution.py:164
  165.7 2.0 collective-permute-done.35.far
  167.7 2.8 %collective-permute-done.34.next_ = f32[192,128]{1,0:T(8,128)S(1)} collective-permute-done((f32[192,128]{1,0:T(8,128)S(1)}, f32[192,128]{1,0:T(8,128)S(1)}, u32[]{:S(2)}, u32[]{:S(2)}) %collective-permute-start.34) | collective-permute-done | bytes 98336 | tf_op jit(solution)/shard_map/ppermute | solution.py:181
  170.4 3.3 %middle.5 = (bf16[128,2048]{1,0:T(8,128)(2,1)S(1)}, f32[320,128]{1,0:T(8,128)S(1)}, f32[256,128]{1,0:T(8,128)S(1)}, f32[256,128]{1,0:T(8,128)S(1)}, f32[192,128]{1,0:T(8,128)S(1)}) custom-call(f32[320,128]{1,0:T(8,128)S(1)} %collective-permute-done.24.near_ref.zero, f32[256,128]{1,0:T(8,128)S(1)} %get-tuple-element.63.own, ...), custom_call_target="tpu_custom_call" | custom-call | tf_op jit(solution)/shard_map/middle/pallas_call | solution.py:164
  173.8 2.5 %collective-permute-start.37 = (f32[256,128]{1,0:T(8,128)S(1)}, f32[256,128]{1,0:T(8,128)S(1)}, u32[]{:S(2)}, u32[]{:S(2)}) collective-permute-start(f32[256,128]{1,0:T(8,128)S(1)} %get-tuple-element.68), channel_id=1, source_target_pairs={{0,2},{1,3},{2,0},{3,1},{4,6},{5,7},{6,4},{7,5},{8,10},{9,11},{10,... | collective-permute-start | bytes 393224 | tf_op jit(solution)/shard_map/ppermute | solution.py:181
  176.3 1.9 collective-permute-start.38
  178.2 7.8 %collective-permute-done.37.next_ref = f32[256,128]{1,0:T(8,128)S(1)} collective-permute-done((f32[256,128]{1,0:T(8,128)S(1)}, f32[256,128]{1,0:T(8,128)S(1)}, u32[]{:S(2)}, u32[]{:S(2)}) %collective-permute-start.37) | collective-permute-done | bytes 131104 | tf_op jit(solution)/shard_map/ppermute | solution.py:181
  186.0 4.2 %collective-permute-start.39 = (f32[192,128]{1,0:T(8,128)S(1)}, f32[192,128]{1,0:T(8,128)S(1)}, u32[]{:S(2)}, u32[]{:S(2)}) collective-permute-start(f32[192,128]{1,0:T(8,128)S(1)} %get-tuple-element.71.kept_ref), channel_id=1, source_target_pairs={{0,6},{1,7},{2,4},{3,5},{4,2},{5,3},{6,0},{7,1},{8,14},{9,15},{10,... | collective-permute-start | bytes 294920 | tf_op jit(solution)/shard_map/ppermute | solution.py:181
  190.3 2.7 %collective-permute-done.39.arrived_ref.refs_0_ = f32[192,128]{1,0:T(8,128)S(1)} collective-permute-done((f32[192,128]{1,0:T(8,128)S(1)}, f32[192,128]{1,0:T(8,128)S(1)}, u32[]{:S(2)}, u32[]{:S(2)}) %collective-permute-start.39) | collective-permute-done | bytes 98336 | tf_op jit(solution)/shard_map/ppermute | solution.py:181
  193.1 4.4 %collective-permute-done.40.arrived_ref.refs_1_ = f32[160,128]{1,0:T(8,128)S(1)} collective-permute-done((f32[160,128]{1,0:T(8,128)S(1)}, f32[160,128]{1,0:T(8,128)S(1)}, u32[]{:S(2)}, u32[]{:S(2)}) %collective-permute-start.40) | collective-permute-done | bytes 81952 | tf_op jit(solution)/shard_map/ppermute | solution.py:181
  198.1 5.0 %collective-permute-done.41.arrived_ref.refs_2_ = f32[128,128]{1,0:T(8,128)S(1)} collective-permute-done((f32[128,128]{1,0:T(8,128)S(1)}, f32[128,128]{1,0:T(8,128)S(1)}, u32[]{:S(2)}, u32[]{:S(2)}) %collective-permute-start.41) | collective-permute-done | bytes 65568 | tf_op jit(solution)/shard_map/ppermute | solution.py:181
  204.4 3.9 %collective-permute-done.43.arrived_ref.refs_4_ = f32[64,128]{1,0:T(8,128)S(1)} collective-permute-done((f32[64,128]{1,0:T(8,128)S(1)}, f32[64,128]{1,0:T(8,128)S(1)}, u32[]{:S(2)}, u32[]{:S(2)}) %collective-permute-start.43) | collective-permute-done | bytes 32800 | tf_op jit(solution)/shard_map/ppermute | solution.py:181
  208.3 2.9 %collective-permute-start.44 = (f32[32,128]{1,0:T(8,128)S(1)}, f32[32,128]{1,0:T(8,128)S(1)}, u32[]{:S(2)}, u32[]{:S(2)}) collective-permute-start(f32[32,128]{1,0:T(8,128)S(1)} %add.39), channel_id=1, source_target_pairs={{0,192},{32,224},{64,128},{96,160},{128,64},{160,96},{192,0},{224,... | collective-permute-start | bytes 49160 | tf_op jit(solution)/shard_map/ppermute | solution.py:181
  211.3 2.0 collective-permute-done.44.refs_5_
  213.3 2.5 %collective-permute-start.45 = (f32[256,128]{1,0:T(8,128)S(1)}, f32[256,128]{1,0:T(8,128)S(1)}, u32[]{:S(2)}, u32[]{:S(2)}) collective-permute-start(f32[256,128]{1,0:T(8,128)S(1)} %get-tuple-element.72.refs_1_), channel_id=1, source_target_pairs={{0,1},{1,0},{2,3},{3,2},{4,5},{5,4},{6,7},{7,6},{8,9},{9,8},{10,11... | collective-permute-start | bytes 393224 | tf_op jit(solution)/shard_map/ppermute | solution.py:181
  215.8 1.9 collective-permute-start.47
  217.7 2.7 %local.7.refs_5_ = f32[128,2048]{1,0:T(8,128)S(1)} custom-call(bf16[128,2048]{1,0:T(8,128)(2,1)S(1)} %get-tuple-element.74.state_ref, bf16[2048,512]{1,0:T(8,128)(2,1)S(1)} %copy-done.3, bf16[2,2048,128]{2,1,0:T(8,128)(2,1)S(1)} %copy-done.5, bf16[2,2048,128]{2,1,0:T(8,128)(2,1)S(1)} %copy-done.7), custom_call_target="tpu_custom_call" | custom-call | tf_op jit(solution)/shard_map/local/pallas_call | solution.py:164
  220.4 2.0 collective-permute-done.47.refs_4_
  222.4 2.8 %collective-permute-done.46.refs_3_ = f32[192,128]{1,0:T(8,128)S(1)} collective-permute-done((f32[192,128]{1,0:T(8,128)S(1)}, f32[192,128]{1,0:T(8,128)S(1)}, u32[]{:S(2)}, u32[]{:S(2)}) %collective-permute-start.46) | collective-permute-done | bytes 98336 | tf_op jit(solution)/shard_map/ppermute | solution.py:181
  225.2 2.8 %last.1 = bf16[128,2048]{1,0:T(8,128)(2,1)} custom-call(f32[320,128]{1,0:T(8,128)S(1)} %collective-permute-done.36.near_ref.refs_0_, f32[256,128]{1,0:T(8,128)S(1)} %get-tuple-element.72.refs_1_, f32[256,128]{1,0:T(8,128)S(1)} %collective-permute-done.45.refs_2_, f32[192,128]{1,0:T(8,128)S(1)} %collective-permute-done.46.refs_3_, ...), custom_call_target="tpu_custom_call" | custom-call | tf_op jit(solution)/shard_map/last/pallas_call | solution.py:164
  (89 shorter events, 17.2 us)
Async XLA Ops:
  0.0 2.2 copy-start
  2.2 1.0 copy-start.8
  3.2 49.7 %copy-start.3 = (bf16[2048,512]{1,0:T(8,128)(2,1)S(1)}, bf16[2048,512]{1,0:T(8,128)(2,1)}, u32[]{:S(2)}) copy-start(bf16[2048,512]{1,0:T(8,128)(2,1)} %leaves_ref.7) | copy-start | bytes 6291460
  3.2 57.1 %copy-start.2 = (bf16[8,2048,128]{2,1,0:T(8,128)(2,1)S(1)}, bf16[8,2048,128]{2,1,0:T(8,128)(2,1)}, u32[]{:S(2)}) copy-start(bf16[8,2048,128]{2,1,0:T(8,128)(2,1)} %refs_6_.1) | copy-start | bytes 12582916
  4.5 55.8 %copy-start.1 = (bf16[8,2048,128]{2,1,0:T(8,128)(2,1)S(1)}, bf16[8,2048,128]{2,1,0:T(8,128)(2,1)}, u32[]{:S(2)}) copy-start(bf16[8,2048,128]{2,1,0:T(8,128)(2,1)} %v_ref.14) | copy-start | bytes 12582916
  4.5 15.3 %collective-permute-start = (f32[320,128]{1,0:T(8,128)S(1)}, f32[320,128]{1,0:T(8,128)S(1)}, u32[]{:S(2)}, u32[]{:S(2)}) collective-permute-start(f32[320,128]{1,0:T(8,128)S(1)} %get-tuple-element.40), channel_id=1, source_target_pairs={{0,1},{1,0},{2,3},{3,2},{4,5},{5,4},{6,7},{7,6},{8,9},{9,8},{10,11... | collective-permute-start | bytes 491528 | tf_op jit(solution)/shard_map/ppermute | solution.py:181
  6.5 13.3 %collective-permute-start.1 = (f32[256,128]{1,0:T(8,128)S(1)}, f32[256,128]{1,0:T(8,128)S(1)}, u32[]{:S(2)}, u32[]{:S(2)}) collective-permute-start(f32[256,128]{1,0:T(8,128)S(1)} %get-tuple-element.42), channel_id=1, source_target_pairs={{0,2},{1,3},{2,0},{3,1},{4,6},{5,7},{6,4},{7,5},{8,10},{9,11},{10,... | collective-permute-start | bytes 393224 | tf_op jit(solution)/shard_map/ppermute | solution.py:181
  9.8 10.0 %collective-permute-start.2 = (f32[256,128]{1,0:T(8,128)S(1)}, f32[256,128]{1,0:T(8,128)S(1)}, u32[]{:S(2)}, u32[]{:S(2)}) collective-permute-start(f32[256,128]{1,0:T(8,128)S(1)} %get-tuple-element.43), channel_id=1, source_target_pairs={{0,3},{1,2},{2,1},{3,0},{4,7},{5,6},{6,5},{7,4},{8,11},{9,10},{10,... | collective-permute-start | bytes 393224 | tf_op jit(solution)/shard_map/ppermute | solution.py:181
  19.8 8.8 %collective-permute-start.3 = (f32[192,128]{1,0:T(8,128)S(1)}, f32[192,128]{1,0:T(8,128)S(1)}, u32[]{:S(2)}, u32[]{:S(2)}) collective-permute-start(f32[192,128]{1,0:T(8,128)S(1)} %get-tuple-element.45.kept_ref), channel_id=1, source_target_pairs={{0,6},{1,7},{2,4},{3,5},{4,2},{5,3},{6,0},{7,1},{8,14},{9,15},{10,... | collective-permute-start | bytes 294920 | tf_op jit(solution)/shard_map/ppermute | solution.py:181
  28.7 4.5 %collective-permute-start.4 = (f32[160,128]{1,0:T(8,128)S(1)}, f32[160,128]{1,0:T(8,128)S(1)}, u32[]{:S(2)}, u32[]{:S(2)}) collective-permute-start(f32[160,128]{1,0:T(8,128)S(1)} %add.20.kept_ref), channel_id=1, source_target_pairs={{0,8},{1,9},{2,10},{3,11},{4,12},{5,13},{6,14},{7,15},{8,0},{9,1},... | collective-permute-start | bytes 245768 | tf_op jit(solution)/shard_map/ppermute | solution.py:181
  33.2 5.6 %collective-permute-start.5 = (f32[128,128]{1,0:T(8,128)S(1)}, f32[128,128]{1,0:T(8,128)S(1)}, u32[]{:S(2)}, u32[]{:S(2)}) collective-permute-start(f32[128,128]{1,0:T(8,128)S(1)} %add.21.kept_ref), channel_id=1, source_target_pairs={{0,24},{1,25},{2,26},{3,27},{4,28},{5,29},{6,30},{7,31},{8,16},{9,... | collective-permute-start | bytes 196616 | tf_op jit(solution)/shard_map/ppermute | solution.py:181
  38.8 1.3 collective-permute-start.6
  40.1 3.9 %collective-permute-start.7 = (f32[64,128]{1,0:T(8,128)S(1)}, f32[64,128]{1,0:T(8,128)S(1)}, u32[]{:S(2)}, u32[]{:S(2)}) collective-permute-start(f32[64,128]{1,0:T(8,128)S(1)} %add.23.kept_ref), channel_id=1, source_target_pairs={{0,64},{32,96},{64,0},{96,32},{128,192},{160,224},{192,128},{224,1... | collective-permute-start | bytes 98312 | tf_op jit(solution)/shard_map/ppermute | solution.py:181
  44.0 4.9 %collective-permute-start.8 = (f32[32,128]{1,0:T(8,128)S(1)}, f32[32,128]{1,0:T(8,128)S(1)}, u32[]{:S(2)}, u32[]{:S(2)}) collective-permute-start(f32[32,128]{1,0:T(8,128)S(1)} %add.24), channel_id=1, source_target_pairs={{0,192},{32,224},{64,128},{96,160},{128,64},{160,96},{192,0},{224,... | collective-permute-start | bytes 49160 | tf_op jit(solution)/shard_map/ppermute | solution.py:181
  49.0 11.3 %collective-permute-start.9 = (f32[256,128]{1,0:T(8,128)S(1)}, f32[256,128]{1,0:T(8,128)S(1)}, u32[]{:S(2)}, u32[]{:S(2)}) collective-permute-start(f32[256,128]{1,0:T(8,128)S(1)} %get-tuple-element.46.own), channel_id=1, source_target_pairs={{0,1},{1,0},{2,3},{3,2},{4,5},{5,4},{6,7},{7,6},{8,9},{9,8},{10,11... | collective-permute-start | bytes 393224 | tf_op jit(solution)/shard_map/ppermute | solution.py:181
  50.3 8.9 %collective-permute-start.11 = (f32[192,128]{1,0:T(8,128)S(1)}, f32[192,128]{1,0:T(8,128)S(1)}, u32[]{:S(2)}, u32[]{:S(2)}) collective-permute-start(f32[192,128]{1,0:T(8,128)S(1)} %get-tuple-element.47), channel_id=1, source_target_pairs={{0,3},{1,2},{2,1},{3,0},{4,7},{5,6},{6,5},{7,4},{8,11},{9,10},{10,... | collective-permute-start | bytes 294920 | tf_op jit(solution)/shard_map/ppermute | solution.py:181
  53.0 7.3 %collective-permute-start.10 = (f32[192,128]{1,0:T(8,128)S(1)}, f32[192,128]{1,0:T(8,128)S(1)}, u32[]{:S(2)}, u32[]{:S(2)}) collective-permute-start(f32[192,128]{1,0:T(8,128)S(1)} %get-tuple-element.47), channel_id=1, source_target_pairs={{0,2},{1,3},{2,0},{3,1},{4,6},{5,7},{6,4},{7,5},{8,10},{9,11},{10,... | collective-permute-start | bytes 294920 | tf_op jit(solution)/shard_map/ppermute | solution.py:181
  53.0 1.2 copy-start.4
  54.2 1.2 copy-start.6
  55.4 1.0 copy-start.9
  59.2 49.0 %copy-start.5 = (bf16[2,2048,128]{2,1,0:T(8,128)(2,1)S(1)}, bf16[2,2048,128]{2,1,0:T(8,128)(2,1)}, u32[]{:S(2)}) copy-start(bf16[2,2048,128]{2,1,0:T(8,128)(2,1)} %u_ref.13) | copy-start | bytes 3145732
  59.2 49.0 %copy-start.7 = (bf16[2,2048,128]{2,1,0:T(8,128)(2,1)S(1)}, bf16[2,2048,128]{2,1,0:T(8,128)(2,1)}, u32[]{:S(2)}) copy-start(bf16[2,2048,128]{2,1,0:T(8,128)(2,1)} %v_ref.15) | copy-start | bytes 3145732
  63.6 12.3 %collective-permute-start.12 = (f32[320,128]{1,0:T(8,128)S(1)}, f32[320,128]{1,0:T(8,128)S(1)}, u32[]{:S(2)}, u32[]{:S(2)}) collective-permute-start(f32[320,128]{1,0:T(8,128)S(1)} %get-tuple-element.48), channel_id=1, source_target_pairs={{0,1},{1,0},{2,3},{3,2},{4,5},{5,4},{6,7},{7,6},{8,9},{9,8},{10,11... | collective-permute-start | bytes 491528 | tf_op jit(solution)/shard_map/ppermute | solution.py:181
  64.4 11.5 %collective-permute-start.13 = (f32[256,128]{1,0:T(8,128)S(1)}, f32[256,128]{1,0:T(8,128)S(1)}, u32[]{:S(2)}, u32[]{:S(2)}) collective-permute-start(f32[256,128]{1,0:T(8,128)S(1)} %get-tuple-element.50), channel_id=1, source_target_pairs={{0,2},{1,3},{2,0},{3,1},{4,6},{5,7},{6,4},{7,5},{8,10},{9,11},{10,... | collective-permute-start | bytes 393224 | tf_op jit(solution)/shard_map/ppermute | solution.py:181
  66.4 9.5 %collective-permute-start.14 = (f32[256,128]{1,0:T(8,128)S(1)}, f32[256,128]{1,0:T(8,128)S(1)}, u32[]{:S(2)}, u32[]{:S(2)}) collective-permute-start(f32[256,128]{1,0:T(8,128)S(1)} %get-tuple-element.51), channel_id=1, source_target_pairs={{0,3},{1,2},{2,1},{3,0},{4,7},{5,6},{6,5},{7,4},{8,11},{9,10},{10,... | collective-permute-start | bytes 393224 | tf_op jit(solution)/shard_map/ppermute | solution.py:181
  75.9 7.6 %collective-permute-start.15 = (f32[192,128]{1,0:T(8,128)S(1)}, f32[192,128]{1,0:T(8,128)S(1)}, u32[]{:S(2)}, u32[]{:S(2)}) collective-permute-start(f32[192,128]{1,0:T(8,128)S(1)} %get-tuple-element.53.kept_ref), channel_id=1, source_target_pairs={{0,6},{1,7},{2,4},{3,5},{4,2},{5,3},{6,0},{7,1},{8,14},{9,15},{10,... | collective-permute-start | bytes 294920 | tf_op jit(solution)/shard_map/ppermute | solution.py:181
  83.5 4.5 %collective-permute-start.16 = (f32[160,128]{1,0:T(8,128)S(1)}, f32[160,128]{1,0:T(8,128)S(1)}, u32[]{:S(2)}, u32[]{:S(2)}) collective-permute-start(f32[160,128]{1,0:T(8,128)S(1)} %add.25.kept_ref), channel_id=1, source_target_pairs={{0,8},{1,9},{2,10},{3,11},{4,12},{5,13},{6,14},{7,15},{8,0},{9,1},... | collective-permute-start | bytes 245768 | tf_op jit(solution)/shard_map/ppermute | solution.py:181
  88.0 5.6 %collective-permute-start.17 = (f32[128,128]{1,0:T(8,128)S(1)}, f32[128,128]{1,0:T(8,128)S(1)}, u32[]{:S(2)}, u32[]{:S(2)}) collective-permute-start(f32[128,128]{1,0:T(8,128)S(1)} %add.26.kept_ref), channel_id=1, source_target_pairs={{0,24},{1,25},{2,26},{3,27},{4,28},{5,29},{6,30},{7,31},{8,16},{9,... | collective-permute-start | bytes 196616 | tf_op jit(solution)/shard_map/ppermute | solution.py:181
  93.6 1.3 collective-permute-start.18
  94.9 3.9 %collective-permute-start.19 = (f32[64,128]{1,0:T(8,128)S(1)}, f32[64,128]{1,0:T(8,128)S(1)}, u32[]{:S(2)}, u32[]{:S(2)}) collective-permute-start(f32[64,128]{1,0:T(8,128)S(1)} %add.28.kept_ref), channel_id=1, source_target_pairs={{0,64},{32,96},{64,0},{96,32},{128,192},{160,224},{192,128},{224,1... | collective-permute-start | bytes 98312 | tf_op jit(solution)/shard_map/ppermute | solution.py:181
  98.8 4.9 %collective-permute-start.20 = (f32[32,128]{1,0:T(8,128)S(1)}, f32[32,128]{1,0:T(8,128)S(1)}, u32[]{:S(2)}, u32[]{:S(2)}) collective-permute-start(f32[32,128]{1,0:T(8,128)S(1)} %add.29), channel_id=1, source_target_pairs={{0,192},{32,224},{64,128},{96,160},{128,64},{160,96},{192,0},{224,... | collective-permute-start | bytes 49160 | tf_op jit(solution)/shard_map/ppermute | solution.py:181
  103.8 11.8 %collective-permute-start.21 = (f32[256,128]{1,0:T(8,128)S(1)}, f32[256,128]{1,0:T(8,128)S(1)}, u32[]{:S(2)}, u32[]{:S(2)}) collective-permute-start(f32[256,128]{1,0:T(8,128)S(1)} %get-tuple-element.54.own), channel_id=1, source_target_pairs={{0,1},{1,0},{2,3},{3,2},{4,5},{5,4},{6,7},{7,6},{8,9},{9,8},{10,11... | collective-permute-start | bytes 393224 | tf_op jit(solution)/shard_map/ppermute | solution.py:181
  106.2 6.6 %collective-permute-start.23 = (f32[192,128]{1,0:T(8,128)S(1)}, f32[192,128]{1,0:T(8,128)S(1)}, u32[]{:S(2)}, u32[]{:S(2)}) collective-permute-start(f32[192,128]{1,0:T(8,128)S(1)} %get-tuple-element.55), channel_id=1, source_target_pairs={{0,3},{1,2},{2,1},{3,0},{4,7},{5,6},{6,5},{7,4},{8,11},{9,10},{10,... | collective-permute-start | bytes 294920 | tf_op jit(solution)/shard_map/ppermute | solution.py:181
  108.2 7.4 %collective-permute-start.22 = (f32[192,128]{1,0:T(8,128)S(1)}, f32[192,128]{1,0:T(8,128)S(1)}, u32[]{:S(2)}, u32[]{:S(2)}) collective-permute-start(f32[192,128]{1,0:T(8,128)S(1)} %get-tuple-element.55), channel_id=1, source_target_pairs={{0,2},{1,3},{2,0},{3,1},{4,6},{5,7},{6,4},{7,5},{8,10},{9,11},{10,... | collective-permute-start | bytes 294920 | tf_op jit(solution)/shard_map/ppermute | solution.py:181
  118.8 12.3 %collective-permute-start.24 = (f32[320,128]{1,0:T(8,128)S(1)}, f32[320,128]{1,0:T(8,128)S(1)}, u32[]{:S(2)}, u32[]{:S(2)}) collective-permute-start(f32[320,128]{1,0:T(8,128)S(1)} %get-tuple-element.57), channel_id=1, source_target_pairs={{0,1},{1,0},{2,3},{3,2},{4,5},{5,4},{6,7},{7,6},{8,9},{9,8},{10,11... | collective-permute-start | bytes 491528 | tf_op jit(solution)/shard_map/ppermute | solution.py:181
  118.9 12.2 %collective-permute-start.25 = (f32[256,128]{1,0:T(8,128)S(1)}, f32[256,128]{1,0:T(8,128)S(1)}, u32[]{:S(2)}, u32[]{:S(2)}) collective-permute-start(f32[256,128]{1,0:T(8,128)S(1)} %get-tuple-element.59), channel_id=1, source_target_pairs={{0,2},{1,3},{2,0},{3,1},{4,6},{5,7},{6,4},{7,5},{8,10},{9,11},{10,... | collective-permute-start | bytes 393224 | tf_op jit(solution)/shard_map/ppermute | solution.py:181
  121.5 9.6 %collective-permute-start.26 = (f32[256,128]{1,0:T(8,128)S(1)}, f32[256,128]{1,0:T(8,128)S(1)}, u32[]{:S(2)}, u32[]{:S(2)}) collective-permute-start(f32[256,128]{1,0:T(8,128)S(1)} %get-tuple-element.60), channel_id=1, source_target_pairs={{0,3},{1,2},{2,1},{3,0},{4,7},{5,6},{6,5},{7,4},{8,11},{9,10},{10,... | collective-permute-start | bytes 393224 | tf_op jit(solution)/shard_map/ppermute | solution.py:181
  131.2 7.0 %collective-permute-start.27 = (f32[192,128]{1,0:T(8,128)S(1)}, f32[192,128]{1,0:T(8,128)S(1)}, u32[]{:S(2)}, u32[]{:S(2)}) collective-permute-start(f32[192,128]{1,0:T(8,128)S(1)} %get-tuple-element.62.kept_ref), channel_id=1, source_target_pairs={{0,6},{1,7},{2,4},{3,5},{4,2},{5,3},{6,0},{7,1},{8,14},{9,15},{10,... | collective-permute-start | bytes 294920 | tf_op jit(solution)/shard_map/ppermute | solution.py:181
  138.2 4.5 %collective-permute-start.28 = (f32[160,128]{1,0:T(8,128)S(1)}, f32[160,128]{1,0:T(8,128)S(1)}, u32[]{:S(2)}, u32[]{:S(2)}) collective-permute-start(f32[160,128]{1,0:T(8,128)S(1)} %add.30.kept_ref), channel_id=1, source_target_pairs={{0,8},{1,9},{2,10},{3,11},{4,12},{5,13},{6,14},{7,15},{8,0},{9,1},... | collective-permute-start | bytes 245768 | tf_op jit(solution)/shard_map/ppermute | solution.py:181
  142.8 5.6 %collective-permute-start.29 = (f32[128,128]{1,0:T(8,128)S(1)}, f32[128,128]{1,0:T(8,128)S(1)}, u32[]{:S(2)}, u32[]{:S(2)}) collective-permute-start(f32[128,128]{1,0:T(8,128)S(1)} %add.31.kept_ref), channel_id=1, source_target_pairs={{0,24},{1,25},{2,26},{3,27},{4,28},{5,29},{6,30},{7,31},{8,16},{9,... | collective-permute-start | bytes 196616 | tf_op jit(solution)/shard_map/ppermute | solution.py:181
  148.4 1.3 collective-permute-start.30
  149.7 3.9 %collective-permute-start.31 = (f32[64,128]{1,0:T(8,128)S(1)}, f32[64,128]{1,0:T(8,128)S(1)}, u32[]{:S(2)}, u32[]{:S(2)}) collective-permute-start(f32[64,128]{1,0:T(8,128)S(1)} %add.33.kept_ref), channel_id=1, source_target_pairs={{0,64},{32,96},{64,0},{96,32},{128,192},{160,224},{192,128},{224,1... | collective-permute-start | bytes 98312 | tf_op jit(solution)/shard_map/ppermute | solution.py:181
  153.6 4.9 %collective-permute-start.32 = (f32[32,128]{1,0:T(8,128)S(1)}, f32[32,128]{1,0:T(8,128)S(1)}, u32[]{:S(2)}, u32[]{:S(2)}) collective-permute-start(f32[32,128]{1,0:T(8,128)S(1)} %add.34), channel_id=1, source_target_pairs={{0,192},{32,224},{64,128},{96,160},{128,64},{160,96},{192,0},{224,... | collective-permute-start | bytes 49160 | tf_op jit(solution)/shard_map/ppermute | solution.py:181
  158.6 11.9 %collective-permute-start.33 = (f32[256,128]{1,0:T(8,128)S(1)}, f32[256,128]{1,0:T(8,128)S(1)}, u32[]{:S(2)}, u32[]{:S(2)}) collective-permute-start(f32[256,128]{1,0:T(8,128)S(1)} %get-tuple-element.63.own), channel_id=1, source_target_pairs={{0,1},{1,0},{2,3},{3,2},{4,5},{5,4},{6,7},{7,6},{8,9},{9,8},{10,11... | collective-permute-start | bytes 393224 | tf_op jit(solution)/shard_map/ppermute | solution.py:181
  161.0 6.6 %collective-permute-start.35 = (f32[192,128]{1,0:T(8,128)S(1)}, f32[192,128]{1,0:T(8,128)S(1)}, u32[]{:S(2)}, u32[]{:S(2)}) collective-permute-start(f32[192,128]{1,0:T(8,128)S(1)} %get-tuple-element.64), channel_id=1, source_target_pairs={{0,3},{1,2},{2,1},{3,0},{4,7},{5,6},{6,5},{7,4},{8,11},{9,10},{10,... | collective-permute-start | bytes 294920 | tf_op jit(solution)/shard_map/ppermute | solution.py:181
  163.0 7.5 %collective-permute-start.34 = (f32[192,128]{1,0:T(8,128)S(1)}, f32[192,128]{1,0:T(8,128)S(1)}, u32[]{:S(2)}, u32[]{:S(2)}) collective-permute-start(f32[192,128]{1,0:T(8,128)S(1)} %get-tuple-element.64), channel_id=1, source_target_pairs={{0,2},{1,3},{2,0},{3,1},{4,6},{5,7},{6,4},{7,5},{8,10},{9,11},{10,... | collective-permute-start | bytes 294920 | tf_op jit(solution)/shard_map/ppermute | solution.py:181
  173.7 12.3 %collective-permute-start.36 = (f32[320,128]{1,0:T(8,128)S(1)}, f32[320,128]{1,0:T(8,128)S(1)}, u32[]{:S(2)}, u32[]{:S(2)}) collective-permute-start(f32[320,128]{1,0:T(8,128)S(1)} %get-tuple-element.66), channel_id=1, source_target_pairs={{0,1},{1,0},{2,3},{3,2},{4,5},{5,4},{6,7},{7,6},{8,9},{9,8},{10,11... | collective-permute-start | bytes 491528 | tf_op jit(solution)/shard_map/ppermute | solution.py:181
  173.8 12.2 %collective-permute-start.37 = (f32[256,128]{1,0:T(8,128)S(1)}, f32[256,128]{1,0:T(8,128)S(1)}, u32[]{:S(2)}, u32[]{:S(2)}) collective-permute-start(f32[256,128]{1,0:T(8,128)S(1)} %get-tuple-element.68), channel_id=1, source_target_pairs={{0,2},{1,3},{2,0},{3,1},{4,6},{5,7},{6,4},{7,5},{8,10},{9,11},{10,... | collective-permute-start | bytes 393224 | tf_op jit(solution)/shard_map/ppermute | solution.py:181
  176.3 9.7 %collective-permute-start.38 = (f32[256,128]{1,0:T(8,128)S(1)}, f32[256,128]{1,0:T(8,128)S(1)}, u32[]{:S(2)}, u32[]{:S(2)}) collective-permute-start(f32[256,128]{1,0:T(8,128)S(1)} %get-tuple-element.69), channel_id=1, source_target_pairs={{0,3},{1,2},{2,1},{3,0},{4,7},{5,6},{6,5},{7,4},{8,11},{9,10},{10,... | collective-permute-start | bytes 393224 | tf_op jit(solution)/shard_map/ppermute | solution.py:181
  186.0 6.9 %collective-permute-start.39 = (f32[192,128]{1,0:T(8,128)S(1)}, f32[192,128]{1,0:T(8,128)S(1)}, u32[]{:S(2)}, u32[]{:S(2)}) collective-permute-start(f32[192,128]{1,0:T(8,128)S(1)} %get-tuple-element.71.kept_ref), channel_id=1, source_target_pairs={{0,6},{1,7},{2,4},{3,5},{4,2},{5,3},{6,0},{7,1},{8,14},{9,15},{10,... | collective-permute-start | bytes 294920 | tf_op jit(solution)/shard_map/ppermute | solution.py:181
  193.0 4.5 %collective-permute-start.40 = (f32[160,128]{1,0:T(8,128)S(1)}, f32[160,128]{1,0:T(8,128)S(1)}, u32[]{:S(2)}, u32[]{:S(2)}) collective-permute-start(f32[160,128]{1,0:T(8,128)S(1)} %add.35.kept_ref), channel_id=1, source_target_pairs={{0,8},{1,9},{2,10},{3,11},{4,12},{5,13},{6,14},{7,15},{8,0},{9,1},... | collective-permute-start | bytes 245768 | tf_op jit(solution)/shard_map/ppermute | solution.py:181
  197.5 5.6 %collective-permute-start.41 = (f32[128,128]{1,0:T(8,128)S(1)}, f32[128,128]{1,0:T(8,128)S(1)}, u32[]{:S(2)}, u32[]{:S(2)}) collective-permute-start(f32[128,128]{1,0:T(8,128)S(1)} %add.36.kept_ref), channel_id=1, source_target_pairs={{0,24},{1,25},{2,26},{3,27},{4,28},{5,29},{6,30},{7,31},{8,16},{9,... | collective-permute-start | bytes 196616 | tf_op jit(solution)/shard_map/ppermute | solution.py:181
  203.1 1.3 collective-permute-start.42
  204.4 3.9 %collective-permute-start.43 = (f32[64,128]{1,0:T(8,128)S(1)}, f32[64,128]{1,0:T(8,128)S(1)}, u32[]{:S(2)}, u32[]{:S(2)}) collective-permute-start(f32[64,128]{1,0:T(8,128)S(1)} %add.38.kept_ref), channel_id=1, source_target_pairs={{0,64},{32,96},{64,0},{96,32},{128,192},{160,224},{192,128},{224,1... | collective-permute-start | bytes 98312 | tf_op jit(solution)/shard_map/ppermute | solution.py:181
  208.3 4.9 %collective-permute-start.44 = (f32[32,128]{1,0:T(8,128)S(1)}, f32[32,128]{1,0:T(8,128)S(1)}, u32[]{:S(2)}, u32[]{:S(2)}) collective-permute-start(f32[32,128]{1,0:T(8,128)S(1)} %add.39), channel_id=1, source_target_pairs={{0,192},{32,224},{64,128},{96,160},{128,64},{160,96},{192,0},{224,... | collective-permute-start | bytes 49160 | tf_op jit(solution)/shard_map/ppermute | solution.py:181
  213.3 11.9 %collective-permute-start.45 = (f32[256,128]{1,0:T(8,128)S(1)}, f32[256,128]{1,0:T(8,128)S(1)}, u32[]{:S(2)}, u32[]{:S(2)}) collective-permute-start(f32[256,128]{1,0:T(8,128)S(1)} %get-tuple-element.72.refs_1_), channel_id=1, source_target_pairs={{0,1},{1,0},{2,3},{3,2},{4,5},{5,4},{6,7},{7,6},{8,9},{9,8},{10,11... | collective-permute-start | bytes 393224 | tf_op jit(solution)/shard_map/ppermute | solution.py:181
  215.8 6.6 %collective-permute-start.47 = (f32[192,128]{1,0:T(8,128)S(1)}, f32[192,128]{1,0:T(8,128)S(1)}, u32[]{:S(2)}, u32[]{:S(2)}) collective-permute-start(f32[192,128]{1,0:T(8,128)S(1)} %get-tuple-element.73), channel_id=1, source_target_pairs={{0,3},{1,2},{2,1},{3,0},{4,7},{5,6},{6,5},{7,4},{8,11},{9,10},{10,... | collective-permute-start | bytes 294920 | tf_op jit(solution)/shard_map/ppermute | solution.py:181
  217.7 7.5 %collective-permute-start.46 = (f32[192,128]{1,0:T(8,128)S(1)}, f32[192,128]{1,0:T(8,128)S(1)}, u32[]{:S(2)}, u32[]{:S(2)}) collective-permute-start(f32[192,128]{1,0:T(8,128)S(1)} %get-tuple-element.73), channel_id=1, source_target_pairs={{0,2},{1,3},{2,0},{3,1},{4,6},{5,7},{6,4},{7,5},{8,10},{9,11},{10,... | collective-permute-start | bytes 294920 | tf_op jit(solution)/shard_map/ppermute | solution.py:181

commit v2 on v1

--- a/solution.py
+++ b/solution.py
@@ -32,7 +32,14 @@
     return half, 2 * half + (lax.div(lo, 2) + lax.div(lo, 4)) % 2
 
 
+def unrolled(count, step):
+    for index in range(count):
+        step(index, 0)
+
+
 def section(index, rows):
+    if isinstance(index, int):
+        return pl.ds(index * rows, rows)
     return pl.ds(pl.multiple_of(index * rows, rows), rows)
 
 
@@ -54,7 +61,7 @@
         parts_ref[level + 1] = both[:, rank:]
         return 0
 
-    lax.fori_loop(0, levels // 2, two_levels, 0)
+    unrolled(levels // 2, two_levels)
     sends[0][pl.ds(0, wide), :] = parts_ref[0]
     sends[1][pl.ds(0, half), :] = parts_ref[1, section(own_half, half), :]
     sends[2][pl.ds(0, half), :] = parts_ref[1, section(1 - own_half, half), :]
@@ -93,7 +100,7 @@
         state_ref[:, rows] = (base_ref[:, rows] + dot_nt(coefs_ref[...], bases)).astype(jnp.bfloat16)
         return 0
 
-    lax.fori_loop(0, state_ref.shape[1] // TILE, tile, 0)
+    unrolled(state_ref.shape[1] // TILE, tile)
 
 
 def middle_kernel(scales, zero, own, near, next_, far, base, u_ref, v_ref, state_ref, *refs):
@@ -119,19 +126,19 @@
             )
             return 0
 
-        lax.fori_loop(0, dev_rows // size, one_node, 0)
+        unrolled(dev_rows // size, one_node)
 
     def one_leaf(index, _):
         rows = section(index, leaf)
         left = [state_ref[:, rows]]
         right = [leaves_ref[rows, :]]
         for level in range(levels):
-            left.append(coefs_ref[level, sibling(lax.div(index, 2**level))])
+            left.append(coefs_ref[level, sibling(index // 2**level)])
             right.append(u_ref[level, rows, :])
         base_ref[:, rows] = dot_nt(jnp.concatenate(left, axis=1), jnp.concatenate(right, axis=1))
         return 0
 
-    lax.fori_loop(0, dev_rows // leaf, one_leaf, 0)
+    unrolled(dev_rows // leaf, one_leaf)
 
 
 def four_kernel(keep_ref, near_ref, next_ref, far_ref, one_ref, out_ref):

time: 228 us -> 224 us (0.982)
  Pallas kernels: 25 us -> 15.2 us
  waiting for transfers between devices: 123 us -> 128 us
    pallas_call x37, Pallas kernels: 25 us -> 15.2 us  [call(): pl.pallas_call(kernel, out_shape=outs, in_specs=[VMEM] * len(args), out_s...]
    ppermute x48, waiting for transfers between devices: 123 us -> 128 us  [from_partner(): return lax.ppermute(value, axis, pairs)]
  transfers between devices with their start and end apart: 48 -> 48, of which waited for: 35 -> 35; matrix products, arithmetic and copies ran while one was open for 0% -> 0% of each run, Pallas kernels for 5% -> 3%
where the time goes in v2:
time: 224 us
  waiting for transfers between devices  128 us (57%)
  starting transfers between devices  73 us (33%)
  Pallas kernels  15.2 us (7%)
  local copies, waits for them, and re-layouts  6.75 us (3%)
    ppermute x48, waiting for transfers between devices, from_partner(): return lax.ppermute(value, axis, pairs)  128 us
    ppermute x48, starting transfers between devices, from_partner(): return lax.ppermute(value, axis, pairs)  73 us
    pallas_call x37, Pallas kernels, call(): pl.pallas_call(kernel, out_shape=outs, in_specs=[VMEM] * len(args), out_s...  15.2 us
    unnamed x20, local copies, waits for them, and re-layouts  6.75 us
  transfers between devices with their start and end apart: 48, of which 35 were waited for; matrix products, arithmetic and copies ran while one was open for 0% of the time, Pallas kernels for 3%

profile of v2, /device:TPU:6, one launch (start us, length us, event | category | flops | bytes accessed | tf_op | source)
XLA Modules:
  0.0 223.5 jit_solution(4799694942829450226)
XLA Ops:
  0.0 2.2 copy-done
  4.0 2.0 collective-permute-start
  6.0 3.3 %collective-permute-start.1 = (f32[256,128]{1,0:T(8,128)S(1)}, f32[256,128]{1,0:T(8,128)S(1)}, u32[]{:S(2)}, u32[]{:S(2)}) collective-permute-start(f32[256,128]{1,0:T(8,128)S(1)} %get-tuple-element.42), channel_id=1, source_target_pairs={{0,2},{1,3},{2,0},{3,1},{4,6},{5,7},{6,4},{7,5},{8,10},{9,11},{10,... | collective-permute-start | bytes 393224 | tf_op jit(solution)/shard_map/ppermute | solution.py:188
  9.3 10.0 %collective-permute-done.1.next_ref = f32[256,128]{1,0:T(8,128)S(1)} collective-permute-done((f32[256,128]{1,0:T(8,128)S(1)}, f32[256,128]{1,0:T(8,128)S(1)}, u32[]{:S(2)}, u32[]{:S(2)}) %collective-permute-start.1) | collective-permute-done | bytes 131104 | tf_op jit(solution)/shard_map/ppermute | solution.py:188
  19.3 6.1 %collective-permute-start.3 = (f32[192,128]{1,0:T(8,128)S(1)}, f32[192,128]{1,0:T(8,128)S(1)}, u32[]{:S(2)}, u32[]{:S(2)}) collective-permute-start(f32[192,128]{1,0:T(8,128)S(1)} %get-tuple-element.45.kept_ref), channel_id=1, source_target_pairs={{0,6},{1,7},{2,4},{3,5},{4,2},{5,3},{6,0},{7,1},{8,14},{9,15},{10,... | collective-permute-start | bytes 294920 | tf_op jit(solution)/shard_map/ppermute | solution.py:188
  25.4 2.7 %collective-permute-done.3.arrived_ref.refs_0_ = f32[192,128]{1,0:T(8,128)S(1)} collective-permute-done((f32[192,128]{1,0:T(8,128)S(1)}, f32[192,128]{1,0:T(8,128)S(1)}, u32[]{:S(2)}, u32[]{:S(2)}) %collective-permute-start.3) | collective-permute-done | bytes 98336 | tf_op jit(solution)/shard_map/ppermute | solution.py:188
  29.1 3.6 %collective-permute-done.4.arrived_ref.refs_1_ = f32[160,128]{1,0:T(8,128)S(1)} collective-permute-done((f32[160,128]{1,0:T(8,128)S(1)}, f32[160,128]{1,0:T(8,128)S(1)}, u32[]{:S(2)}, u32[]{:S(2)}) %collective-permute-start.4) | collective-permute-done | bytes 81952 | tf_op jit(solution)/shard_map/ppermute | solution.py:188
  33.2 5.0 %collective-permute-done.5.arrived_ref.refs_2_ = f32[128,128]{1,0:T(8,128)S(1)} collective-permute-done((f32[128,128]{1,0:T(8,128)S(1)}, f32[128,128]{1,0:T(8,128)S(1)}, u32[]{:S(2)}, u32[]{:S(2)}) %collective-permute-start.5) | collective-permute-done | bytes 65568 | tf_op jit(solution)/shard_map/ppermute | solution.py:188
  39.6 1.6 collective-permute-start.7
  41.1 2.3 %collective-permute-done.7.arrived_ref.refs_4_ = f32[64,128]{1,0:T(8,128)S(1)} collective-permute-done((f32[64,128]{1,0:T(8,128)S(1)}, f32[64,128]{1,0:T(8,128)S(1)}, u32[]{:S(2)}, u32[]{:S(2)}) %collective-permute-start.7) | collective-permute-done | bytes 32800 | tf_op jit(solution)/shard_map/ppermute | solution.py:188
  43.5 3.0 %collective-permute-start.8 = (f32[32,128]{1,0:T(8,128)S(1)}, f32[32,128]{1,0:T(8,128)S(1)}, u32[]{:S(2)}, u32[]{:S(2)}) collective-permute-start(f32[32,128]{1,0:T(8,128)S(1)} %add.24), channel_id=1, source_target_pairs={{0,192},{32,224},{64,128},{96,160},{128,64},{160,96},{192,0},{224,... | collective-permute-start | bytes 49160 | tf_op jit(solution)/shard_map/ppermute | solution.py:188
  46.5 1.9 collective-permute-done.8.refs_5_
  48.5 1.5 collective-permute-start.9
  50.0 2.4 %collective-permute-start.11 = (f32[192,128]{1,0:T(8,128)S(1)}, f32[192,128]{1,0:T(8,128)S(1)}, u32[]{:S(2)}, u32[]{:S(2)}) collective-permute-start(f32[192,128]{1,0:T(8,128)S(1)} %get-tuple-element.47), channel_id=1, source_target_pairs={{0,3},{1,2},{2,1},{3,0},{4,7},{5,6},{6,5},{7,4},{8,11},{9,10},{10,... | collective-permute-start | bytes 294920 | tf_op jit(solution)/shard_map/ppermute | solution.py:188
  55.9 1.4 local.4.base
  57.4 2.4 %collective-permute-done.10.next_ = f32[192,128]{1,0:T(8,128)S(1)} collective-permute-done((f32[192,128]{1,0:T(8,128)S(1)}, f32[192,128]{1,0:T(8,128)S(1)}, u32[]{:S(2)}, u32[]{:S(2)}) %collective-permute-start.10) | collective-permute-done | bytes 98336 | tf_op jit(solution)/shard_map/ppermute | solution.py:188
  59.8 2.1 middle.3
  62.0 2.7 %collective-permute-start.13 = (f32[256,128]{1,0:T(8,128)S(1)}, f32[256,128]{1,0:T(8,128)S(1)}, u32[]{:S(2)}, u32[]{:S(2)}) collective-permute-start(f32[256,128]{1,0:T(8,128)S(1)} %get-tuple-element.50), channel_id=1, source_target_pairs={{0,2},{1,3},{2,0},{3,1},{4,6},{5,7},{6,4},{7,5},{8,10},{9,11},{10,... | collective-permute-start | bytes 393224 | tf_op jit(solution)/shard_map/ppermute | solution.py:188
  64.7 1.7 collective-permute-start.14
  66.3 7.8 %collective-permute-done.13.next_ref = f32[256,128]{1,0:T(8,128)S(1)} collective-permute-done((f32[256,128]{1,0:T(8,128)S(1)}, f32[256,128]{1,0:T(8,128)S(1)}, u32[]{:S(2)}, u32[]{:S(2)}) %collective-permute-start.13) | collective-permute-done | bytes 131104 | tf_op jit(solution)/shard_map/ppermute | solution.py:188
  74.2 4.8 %collective-permute-start.15 = (f32[192,128]{1,0:T(8,128)S(1)}, f32[192,128]{1,0:T(8,128)S(1)}, u32[]{:S(2)}, u32[]{:S(2)}) collective-permute-start(f32[192,128]{1,0:T(8,128)S(1)} %get-tuple-element.53.kept_ref), channel_id=1, source_target_pairs={{0,6},{1,7},{2,4},{3,5},{4,2},{5,3},{6,0},{7,1},{8,14},{9,15},{10,... | collective-permute-start | bytes 294920 | tf_op jit(solution)/shard_map/ppermute | solution.py:188
  79.0 2.7 %collective-permute-done.15.arrived_ref.refs_0_ = f32[192,128]{1,0:T(8,128)S(1)} collective-permute-done((f32[192,128]{1,0:T(8,128)S(1)}, f32[192,128]{1,0:T(8,128)S(1)}, u32[]{:S(2)}, u32[]{:S(2)}) %collective-permute-start.15) | collective-permute-done | bytes 98336 | tf_op jit(solution)/shard_map/ppermute | solution.py:188
  82.1 4.4 %collective-permute-done.16.arrived_ref.refs_1_ = f32[160,128]{1,0:T(8,128)S(1)} collective-permute-done((f32[160,128]{1,0:T(8,128)S(1)}, f32[160,128]{1,0:T(8,128)S(1)}, u32[]{:S(2)}, u32[]{:S(2)}) %collective-permute-start.16) | collective-permute-done | bytes 81952 | tf_op jit(solution)/shard_map/ppermute | solution.py:188
  87.1 5.0 %collective-permute-done.17.arrived_ref.refs_2_ = f32[128,128]{1,0:T(8,128)S(1)} collective-permute-done((f32[128,128]{1,0:T(8,128)S(1)}, f32[128,128]{1,0:T(8,128)S(1)}, u32[]{:S(2)}, u32[]{:S(2)}) %collective-permute-start.17) | collective-permute-done | bytes 65568 | tf_op jit(solution)/shard_map/ppermute | solution.py:188
  93.7 3.6 %collective-permute-done.19.arrived_ref.refs_4_ = f32[64,128]{1,0:T(8,128)S(1)} collective-permute-done((f32[64,128]{1,0:T(8,128)S(1)}, f32[64,128]{1,0:T(8,128)S(1)}, u32[]{:S(2)}, u32[]{:S(2)}) %collective-permute-start.19) | collective-permute-done | bytes 32800 | tf_op jit(solution)/shard_map/ppermute | solution.py:188
  97.3 2.9 %collective-permute-start.20 = (f32[32,128]{1,0:T(8,128)S(1)}, f32[32,128]{1,0:T(8,128)S(1)}, u32[]{:S(2)}, u32[]{:S(2)}) collective-permute-start(f32[32,128]{1,0:T(8,128)S(1)} %add.29), channel_id=1, source_target_pairs={{0,192},{32,224},{64,128},{96,160},{128,64},{160,96},{192,0},{224,... | collective-permute-start | bytes 49160 | tf_op jit(solution)/shard_map/ppermute | solution.py:188
  100.3 2.0 collective-permute-done.20.refs_5_
  102.3 2.4 %collective-permute-start.21 = (f32[256,128]{1,0:T(8,128)S(1)}, f32[256,128]{1,0:T(8,128)S(1)}, u32[]{:S(2)}, u32[]{:S(2)}) collective-permute-start(f32[256,128]{1,0:T(8,128)S(1)} %get-tuple-element.54.own), channel_id=1, source_target_pairs={{0,1},{1,0},{2,3},{3,2},{4,5},{5,4},{6,7},{7,6},{8,9},{9,8},{10,11... | collective-permute-start | bytes 393224 | tf_op jit(solution)/shard_map/ppermute | solution.py:188
  104.6 2.0 collective-permute-start.23
  106.7 1.4 local.5.base
  108.1 3.2 %collective-permute-done.23.far = f32[192,128]{1,0:T(8,128)S(1)} collective-permute-done((f32[192,128]{1,0:T(8,128)S(1)}, f32[192,128]{1,0:T(8,128)S(1)}, u32[]{:S(2)}, u32[]{:S(2)}) %collective-permute-start.23) | collective-permute-done | bytes 98336 | tf_op jit(solution)/shard_map/ppermute | solution.py:188
  111.3 2.8 %collective-permute-done.22.next_ = f32[192,128]{1,0:T(8,128)S(1)} collective-permute-done((f32[192,128]{1,0:T(8,128)S(1)}, f32[192,128]{1,0:T(8,128)S(1)}, u32[]{:S(2)}, u32[]{:S(2)}) %collective-permute-start.22) | collective-permute-done | bytes 98336 | tf_op jit(solution)/shard_map/ppermute | solution.py:188
  114.0 2.1 middle.4
  116.2 2.6 %collective-permute-start.25 = (f32[256,128]{1,0:T(8,128)S(1)}, f32[256,128]{1,0:T(8,128)S(1)}, u32[]{:S(2)}, u32[]{:S(2)}) collective-permute-start(f32[256,128]{1,0:T(8,128)S(1)} %get-tuple-element.59), channel_id=1, source_target_pairs={{0,2},{1,3},{2,0},{3,1},{4,6},{5,7},{6,4},{7,5},{8,10},{9,11},{10,... | collective-permute-start | bytes 393224 | tf_op jit(solution)/shard_map/ppermute | solution.py:188
  118.8 1.8 collective-permute-start.26
  120.6 7.8 %collective-permute-done.25.next_ref = f32[256,128]{1,0:T(8,128)S(1)} collective-permute-done((f32[256,128]{1,0:T(8,128)S(1)}, f32[256,128]{1,0:T(8,128)S(1)}, u32[]{:S(2)}, u32[]{:S(2)}) %collective-permute-start.25) | collective-permute-done | bytes 131104 | tf_op jit(solution)/shard_map/ppermute | solution.py:188
  128.5 4.3 %collective-permute-start.27 = (f32[192,128]{1,0:T(8,128)S(1)}, f32[192,128]{1,0:T(8,128)S(1)}, u32[]{:S(2)}, u32[]{:S(2)}) collective-permute-start(f32[192,128]{1,0:T(8,128)S(1)} %get-tuple-element.62.kept_ref), channel_id=1, source_target_pairs={{0,6},{1,7},{2,4},{3,5},{4,2},{5,3},{6,0},{7,1},{8,14},{9,15},{10,... | collective-permute-start | bytes 294920 | tf_op jit(solution)/shard_map/ppermute | solution.py:188
  132.8 2.7 %collective-permute-done.27.arrived_ref.refs_0_ = f32[192,128]{1,0:T(8,128)S(1)} collective-permute-done((f32[192,128]{1,0:T(8,128)S(1)}, f32[192,128]{1,0:T(8,128)S(1)}, u32[]{:S(2)}, u32[]{:S(2)}) %collective-permute-start.27) | collective-permute-done | bytes 98336 | tf_op jit(solution)/shard_map/ppermute | solution.py:188
  135.6 4.4 %collective-permute-done.28.arrived_ref.refs_1_ = f32[160,128]{1,0:T(8,128)S(1)} collective-permute-done((f32[160,128]{1,0:T(8,128)S(1)}, f32[160,128]{1,0:T(8,128)S(1)}, u32[]{:S(2)}, u32[]{:S(2)}) %collective-permute-start.28) | collective-permute-done | bytes 81952 | tf_op jit(solution)/shard_map/ppermute | solution.py:188
  140.6 5.0 %collective-permute-done.29.arrived_ref.refs_2_ = f32[128,128]{1,0:T(8,128)S(1)} collective-permute-done((f32[128,128]{1,0:T(8,128)S(1)}, f32[128,128]{1,0:T(8,128)S(1)}, u32[]{:S(2)}, u32[]{:S(2)}) %collective-permute-start.29) | collective-permute-done | bytes 65568 | tf_op jit(solution)/shard_map/ppermute | solution.py:188
  147.0 3.9 %collective-permute-done.31.arrived_ref.refs_4_ = f32[64,128]{1,0:T(8,128)S(1)} collective-permute-done((f32[64,128]{1,0:T(8,128)S(1)}, f32[64,128]{1,0:T(8,128)S(1)}, u32[]{:S(2)}, u32[]{:S(2)}) %collective-permute-start.31) | collective-permute-done | bytes 32800 | tf_op jit(solution)/shard_map/ppermute | solution.py:188
  150.9 2.9 %collective-permute-start.32 = (f32[32,128]{1,0:T(8,128)S(1)}, f32[32,128]{1,0:T(8,128)S(1)}, u32[]{:S(2)}, u32[]{:S(2)}) collective-permute-start(f32[32,128]{1,0:T(8,128)S(1)} %add.34), channel_id=1, source_target_pairs={{0,192},{32,224},{64,128},{96,160},{128,64},{160,96},{192,0},{224,... | collective-permute-start | bytes 49160 | tf_op jit(solution)/shard_map/ppermute | solution.py:188
  153.8 2.0 collective-permute-done.32.refs_5_
  155.8 2.5 %collective-permute-start.33 = (f32[256,128]{1,0:T(8,128)S(1)}, f32[256,128]{1,0:T(8,128)S(1)}, u32[]{:S(2)}, u32[]{:S(2)}) collective-permute-start(f32[256,128]{1,0:T(8,128)S(1)} %get-tuple-element.63.own), channel_id=1, source_target_pairs={{0,1},{1,0},{2,3},{3,2},{4,5},{5,4},{6,7},{7,6},{8,9},{9,8},{10,11... | collective-permute-start | bytes 393224 | tf_op jit(solution)/shard_map/ppermute | solution.py:188
  158.3 1.9 collective-permute-start.35
  161.7 3.3 %collective-permute-done.35.far = f32[192,128]{1,0:T(8,128)S(1)} collective-permute-done((f32[192,128]{1,0:T(8,128)S(1)}, f32[192,128]{1,0:T(8,128)S(1)}, u32[]{:S(2)}, u32[]{:S(2)}) %collective-permute-start.35) | collective-permute-done | bytes 98336 | tf_op jit(solution)/shard_map/ppermute | solution.py:188
  164.9 2.8 %collective-permute-done.34.next_ = f32[192,128]{1,0:T(8,128)S(1)} collective-permute-done((f32[192,128]{1,0:T(8,128)S(1)}, f32[192,128]{1,0:T(8,128)S(1)}, u32[]{:S(2)}, u32[]{:S(2)}) %collective-permute-start.34) | collective-permute-done | bytes 98336 | tf_op jit(solution)/shard_map/ppermute | solution.py:188
  167.7 2.1 middle.5
  169.9 2.5 %collective-permute-start.37 = (f32[256,128]{1,0:T(8,128)S(1)}, f32[256,128]{1,0:T(8,128)S(1)}, u32[]{:S(2)}, u32[]{:S(2)}) collective-permute-start(f32[256,128]{1,0:T(8,128)S(1)} %get-tuple-element.68), channel_id=1, source_target_pairs={{0,2},{1,3},{2,0},{3,1},{4,6},{5,7},{6,4},{7,5},{8,10},{9,11},{10,... | collective-permute-start | bytes 393224 | tf_op jit(solution)/shard_map/ppermute | solution.py:188
  172.4 1.9 collective-permute-start.38
  174.3 7.8 %collective-permute-done.37.next_ref = f32[256,128]{1,0:T(8,128)S(1)} collective-permute-done((f32[256,128]{1,0:T(8,128)S(1)}, f32[256,128]{1,0:T(8,128)S(1)}, u32[]{:S(2)}, u32[]{:S(2)}) %collective-permute-start.37) | collective-permute-done | bytes 131104 | tf_op jit(solution)/shard_map/ppermute | solution.py:188
  182.1 4.2 %collective-permute-start.39 = (f32[192,128]{1,0:T(8,128)S(1)}, f32[192,128]{1,0:T(8,128)S(1)}, u32[]{:S(2)}, u32[]{:S(2)}) collective-permute-start(f32[192,128]{1,0:T(8,128)S(1)} %get-tuple-element.71.kept_ref), channel_id=1, source_target_pairs={{0,6},{1,7},{2,4},{3,5},{4,2},{5,3},{6,0},{7,1},{8,14},{9,15},{10,... | collective-permute-start | bytes 294920 | tf_op jit(solution)/shard_map/ppermute | solution.py:188
  186.3 2.7 %collective-permute-done.39.arrived_ref.refs_0_ = f32[192,128]{1,0:T(8,128)S(1)} collective-permute-done((f32[192,128]{1,0:T(8,128)S(1)}, f32[192,128]{1,0:T(8,128)S(1)}, u32[]{:S(2)}, u32[]{:S(2)}) %collective-permute-start.39) | collective-permute-done | bytes 98336 | tf_op jit(solution)/shard_map/ppermute | solution.py:188
  189.1 4.4 %collective-permute-done.40.arrived_ref.refs_1_ = f32[160,128]{1,0:T(8,128)S(1)} collective-permute-done((f32[160,128]{1,0:T(8,128)S(1)}, f32[160,128]{1,0:T(8,128)S(1)}, u32[]{:S(2)}, u32[]{:S(2)}) %collective-permute-start.40) | collective-permute-done | bytes 81952 | tf_op jit(solution)/shard_map/ppermute | solution.py:188
  194.1 5.0 %collective-permute-done.41.arrived_ref.refs_2_ = f32[128,128]{1,0:T(8,128)S(1)} collective-permute-done((f32[128,128]{1,0:T(8,128)S(1)}, f32[128,128]{1,0:T(8,128)S(1)}, u32[]{:S(2)}, u32[]{:S(2)}) %collective-permute-start.41) | collective-permute-done | bytes 65568 | tf_op jit(solution)/shard_map/ppermute | solution.py:188
  200.5 3.9 %collective-permute-done.43.arrived_ref.refs_4_ = f32[64,128]{1,0:T(8,128)S(1)} collective-permute-done((f32[64,128]{1,0:T(8,128)S(1)}, f32[64,128]{1,0:T(8,128)S(1)}, u32[]{:S(2)}, u32[]{:S(2)}) %collective-permute-start.43) | collective-permute-done | bytes 32800 | tf_op jit(solution)/shard_map/ppermute | solution.py:188
  204.4 2.9 %collective-permute-start.44 = (f32[32,128]{1,0:T(8,128)S(1)}, f32[32,128]{1,0:T(8,128)S(1)}, u32[]{:S(2)}, u32[]{:S(2)}) collective-permute-start(f32[32,128]{1,0:T(8,128)S(1)} %add.39), channel_id=1, source_target_pairs={{0,192},{32,224},{64,128},{96,160},{128,64},{160,96},{192,0},{224,... | collective-permute-start | bytes 49160 | tf_op jit(solution)/shard_map/ppermute | solution.py:188
  207.3 2.0 collective-permute-done.44.refs_5_
  209.4 2.5 %collective-permute-start.45 = (f32[256,128]{1,0:T(8,128)S(1)}, f32[256,128]{1,0:T(8,128)S(1)}, u32[]{:S(2)}, u32[]{:S(2)}) collective-permute-start(f32[256,128]{1,0:T(8,128)S(1)} %get-tuple-element.72.refs_1_), channel_id=1, source_target_pairs={{0,1},{1,0},{2,3},{3,2},{4,5},{5,4},{6,7},{7,6},{8,9},{9,8},{10,11... | collective-permute-start | bytes 393224 | tf_op jit(solution)/shard_map/ppermute | solution.py:188
  211.9 1.9 collective-permute-start.47
  213.8 1.4 local.7.refs_5_
  215.2 3.3 %collective-permute-done.47.refs_4_ = f32[192,128]{1,0:T(8,128)S(1)} collective-permute-done((f32[192,128]{1,0:T(8,128)S(1)}, f32[192,128]{1,0:T(8,128)S(1)}, u32[]{:S(2)}, u32[]{:S(2)}) %collective-permute-start.47) | collective-permute-done | bytes 98336 | tf_op jit(solution)/shard_map/ppermute | solution.py:188
  218.5 2.8 %collective-permute-done.46.refs_3_ = f32[192,128]{1,0:T(8,128)S(1)} collective-permute-done((f32[192,128]{1,0:T(8,128)S(1)}, f32[192,128]{1,0:T(8,128)S(1)}, u32[]{:S(2)}, u32[]{:S(2)}) %collective-permute-start.46) | collective-permute-done | bytes 98336 | tf_op jit(solution)/shard_map/ppermute | solution.py:188
  221.2 2.3 %last.1 = bf16[128,2048]{1,0:T(8,128)(2,1)} custom-call(f32[320,128]{1,0:T(8,128)S(1)} %collective-permute-done.36.near_ref.refs_0_, f32[256,128]{1,0:T(8,128)S(1)} %get-tuple-element.72.refs_1_, f32[256,128]{1,0:T(8,128)S(1)} %collective-permute-done.45.refs_2_, f32[192,128]{1,0:T(8,128)S(1)} %collective-permute-done.46.refs_3_, ...), custom_call_target="tpu_custom_call" | custom-call | tf_op jit(solution)/shard_map/last/pallas_call | solution.py:171
  (89 shorter events, 16.5 us)
Async XLA Ops:
  0.0 2.2 copy-start
  2.2 1.0 copy-start.8
  3.2 49.2 %copy-start.3 = (bf16[2048,512]{1,0:T(8,128)(2,1)S(1)}, bf16[2048,512]{1,0:T(8,128)(2,1)}, u32[]{:S(2)}) copy-start(bf16[2048,512]{1,0:T(8,128)(2,1)} %leaves_ref.7) | copy-start | bytes 6291460
  3.2 56.5 %copy-start.2 = (bf16[8,2048,128]{2,1,0:T(8,128)(2,1)S(1)}, bf16[8,2048,128]{2,1,0:T(8,128)(2,1)}, u32[]{:S(2)}) copy-start(bf16[8,2048,128]{2,1,0:T(8,128)(2,1)} %refs_6_.1) | copy-start | bytes 12582916
  4.0 55.8 %copy-start.1 = (bf16[8,2048,128]{2,1,0:T(8,128)(2,1)S(1)}, bf16[8,2048,128]{2,1,0:T(8,128)(2,1)}, u32[]{:S(2)}) copy-start(bf16[8,2048,128]{2,1,0:T(8,128)(2,1)} %v_ref.14) | copy-start | bytes 12582916
  4.0 15.3 %collective-permute-start = (f32[320,128]{1,0:T(8,128)S(1)}, f32[320,128]{1,0:T(8,128)S(1)}, u32[]{:S(2)}, u32[]{:S(2)}) collective-permute-start(f32[320,128]{1,0:T(8,128)S(1)} %get-tuple-element.40), channel_id=1, source_target_pairs={{0,1},{1,0},{2,3},{3,2},{4,5},{5,4},{6,7},{7,6},{8,9},{9,8},{10,11... | collective-permute-start | bytes 491528 | tf_op jit(solution)/shard_map/ppermute | solution.py:188
  6.0 13.2 %collective-permute-start.1 = (f32[256,128]{1,0:T(8,128)S(1)}, f32[256,128]{1,0:T(8,128)S(1)}, u32[]{:S(2)}, u32[]{:S(2)}) collective-permute-start(f32[256,128]{1,0:T(8,128)S(1)} %get-tuple-element.42), channel_id=1, source_target_pairs={{0,2},{1,3},{2,0},{3,1},{4,6},{5,7},{6,4},{7,5},{8,10},{9,11},{10,... | collective-permute-start | bytes 393224 | tf_op jit(solution)/shard_map/ppermute | solution.py:188
  9.3 10.0 %collective-permute-start.2 = (f32[256,128]{1,0:T(8,128)S(1)}, f32[256,128]{1,0:T(8,128)S(1)}, u32[]{:S(2)}, u32[]{:S(2)}) collective-permute-start(f32[256,128]{1,0:T(8,128)S(1)} %get-tuple-element.43), channel_id=1, source_target_pairs={{0,3},{1,2},{2,1},{3,0},{4,7},{5,6},{6,5},{7,4},{8,11},{9,10},{10,... | collective-permute-start | bytes 393224 | tf_op jit(solution)/shard_map/ppermute | solution.py:188
  19.3 8.8 %collective-permute-start.3 = (f32[192,128]{1,0:T(8,128)S(1)}, f32[192,128]{1,0:T(8,128)S(1)}, u32[]{:S(2)}, u32[]{:S(2)}) collective-permute-start(f32[192,128]{1,0:T(8,128)S(1)} %get-tuple-element.45.kept_ref), channel_id=1, source_target_pairs={{0,6},{1,7},{2,4},{3,5},{4,2},{5,3},{6,0},{7,1},{8,14},{9,15},{10,... | collective-permute-start | bytes 294920 | tf_op jit(solution)/shard_map/ppermute | solution.py:188
  28.1 4.5 %collective-permute-start.4 = (f32[160,128]{1,0:T(8,128)S(1)}, f32[160,128]{1,0:T(8,128)S(1)}, u32[]{:S(2)}, u32[]{:S(2)}) collective-permute-start(f32[160,128]{1,0:T(8,128)S(1)} %add.20.kept_ref), channel_id=1, source_target_pairs={{0,8},{1,9},{2,10},{3,11},{4,12},{5,13},{6,14},{7,15},{8,0},{9,1},... | collective-permute-start | bytes 245768 | tf_op jit(solution)/shard_map/ppermute | solution.py:188
  32.7 5.6 %collective-permute-start.5 = (f32[128,128]{1,0:T(8,128)S(1)}, f32[128,128]{1,0:T(8,128)S(1)}, u32[]{:S(2)}, u32[]{:S(2)}) collective-permute-start(f32[128,128]{1,0:T(8,128)S(1)} %add.21.kept_ref), channel_id=1, source_target_pairs={{0,24},{1,25},{2,26},{3,27},{4,28},{5,29},{6,30},{7,31},{8,16},{9,... | collective-permute-start | bytes 196616 | tf_op jit(solution)/shard_map/ppermute | solution.py:188
  38.3 1.3 collective-permute-start.6
  39.6 3.9 %collective-permute-start.7 = (f32[64,128]{1,0:T(8,128)S(1)}, f32[64,128]{1,0:T(8,128)S(1)}, u32[]{:S(2)}, u32[]{:S(2)}) collective-permute-start(f32[64,128]{1,0:T(8,128)S(1)} %add.23.kept_ref), channel_id=1, source_target_pairs={{0,64},{32,96},{64,0},{96,32},{128,192},{160,224},{192,128},{224,1... | collective-permute-start | bytes 98312 | tf_op jit(solution)/shard_map/ppermute | solution.py:188
  43.5 4.9 %collective-permute-start.8 = (f32[32,128]{1,0:T(8,128)S(1)}, f32[32,128]{1,0:T(8,128)S(1)}, u32[]{:S(2)}, u32[]{:S(2)}) collective-permute-start(f32[32,128]{1,0:T(8,128)S(1)} %add.24), channel_id=1, source_target_pairs={{0,192},{32,224},{64,128},{96,160},{128,64},{160,96},{192,0},{224,... | collective-permute-start | bytes 49160 | tf_op jit(solution)/shard_map/ppermute | solution.py:188
  48.5 11.3 %collective-permute-start.9 = (f32[256,128]{1,0:T(8,128)S(1)}, f32[256,128]{1,0:T(8,128)S(1)}, u32[]{:S(2)}, u32[]{:S(2)}) collective-permute-start(f32[256,128]{1,0:T(8,128)S(1)} %get-tuple-element.46.own), channel_id=1, source_target_pairs={{0,1},{1,0},{2,3},{3,2},{4,5},{5,4},{6,7},{7,6},{8,9},{9,8},{10,11... | collective-permute-start | bytes 393224 | tf_op jit(solution)/shard_map/ppermute | solution.py:188
  50.0 7.4 %collective-permute-start.11 = (f32[192,128]{1,0:T(8,128)S(1)}, f32[192,128]{1,0:T(8,128)S(1)}, u32[]{:S(2)}, u32[]{:S(2)}) collective-permute-start(f32[192,128]{1,0:T(8,128)S(1)} %get-tuple-element.47), channel_id=1, source_target_pairs={{0,3},{1,2},{2,1},{3,0},{4,7},{5,6},{6,5},{7,4},{8,11},{9,10},{10,... | collective-permute-start | bytes 294920 | tf_op jit(solution)/shard_map/ppermute | solution.py:188
  52.4 7.3 %collective-permute-start.10 = (f32[192,128]{1,0:T(8,128)S(1)}, f32[192,128]{1,0:T(8,128)S(1)}, u32[]{:S(2)}, u32[]{:S(2)}) collective-permute-start(f32[192,128]{1,0:T(8,128)S(1)} %get-tuple-element.47), channel_id=1, source_target_pairs={{0,2},{1,3},{2,0},{3,1},{4,6},{5,7},{6,4},{7,5},{8,10},{9,11},{10,... | collective-permute-start | bytes 294920 | tf_op jit(solution)/shard_map/ppermute | solution.py:188
  52.5 1.2 copy-start.4
  53.7 1.2 copy-start.6
  54.9 1.0 copy-start.9
  57.4 49.3 %copy-start.5 = (bf16[2,2048,128]{2,1,0:T(8,128)(2,1)S(1)}, bf16[2,2048,128]{2,1,0:T(8,128)(2,1)}, u32[]{:S(2)}) copy-start(bf16[2,2048,128]{2,1,0:T(8,128)(2,1)} %u_ref.13) | copy-start | bytes 3145732
  57.4 49.3 %copy-start.7 = (bf16[2,2048,128]{2,1,0:T(8,128)(2,1)S(1)}, bf16[2,2048,128]{2,1,0:T(8,128)(2,1)}, u32[]{:S(2)}) copy-start(bf16[2,2048,128]{2,1,0:T(8,128)(2,1)} %v_ref.15) | copy-start | bytes 3145732
  61.9 12.3 %collective-permute-start.12 = (f32[320,128]{1,0:T(8,128)S(1)}, f32[320,128]{1,0:T(8,128)S(1)}, u32[]{:S(2)}, u32[]{:S(2)}) collective-permute-start(f32[320,128]{1,0:T(8,128)S(1)} %get-tuple-element.48), channel_id=1, source_target_pairs={{0,1},{1,0},{2,3},{3,2},{4,5},{5,4},{6,7},{7,6},{8,9},{9,8},{10,11... | collective-permute-start | bytes 491528 | tf_op jit(solution)/shard_map/ppermute | solution.py:188
  62.0 12.2 %collective-permute-start.13 = (f32[256,128]{1,0:T(8,128)S(1)}, f32[256,128]{1,0:T(8,128)S(1)}, u32[]{:S(2)}, u32[]{:S(2)}) collective-permute-start(f32[256,128]{1,0:T(8,128)S(1)} %get-tuple-element.50), channel_id=1, source_target_pairs={{0,2},{1,3},{2,0},{3,1},{4,6},{5,7},{6,4},{7,5},{8,10},{9,11},{10,... | collective-permute-start | bytes 393224 | tf_op jit(solution)/shard_map/ppermute | solution.py:188
  64.7 9.5 %collective-permute-start.14 = (f32[256,128]{1,0:T(8,128)S(1)}, f32[256,128]{1,0:T(8,128)S(1)}, u32[]{:S(2)}, u32[]{:S(2)}) collective-permute-start(f32[256,128]{1,0:T(8,128)S(1)} %get-tuple-element.51), channel_id=1, source_target_pairs={{0,3},{1,2},{2,1},{3,0},{4,7},{5,6},{6,5},{7,4},{8,11},{9,10},{10,... | collective-permute-start | bytes 393224 | tf_op jit(solution)/shard_map/ppermute | solution.py:188
  74.2 7.6 %collective-permute-start.15 = (f32[192,128]{1,0:T(8,128)S(1)}, f32[192,128]{1,0:T(8,128)S(1)}, u32[]{:S(2)}, u32[]{:S(2)}) collective-permute-start(f32[192,128]{1,0:T(8,128)S(1)} %get-tuple-element.53.kept_ref), channel_id=1, source_target_pairs={{0,6},{1,7},{2,4},{3,5},{4,2},{5,3},{6,0},{7,1},{8,14},{9,15},{10,... | collective-permute-start | bytes 294920 | tf_op jit(solution)/shard_map/ppermute | solution.py:188
  81.8 4.7 %collective-permute-start.16 = (f32[160,128]{1,0:T(8,128)S(1)}, f32[160,128]{1,0:T(8,128)S(1)}, u32[]{:S(2)}, u32[]{:S(2)}) collective-permute-start(f32[160,128]{1,0:T(8,128)S(1)} %add.25.kept_ref), channel_id=1, source_target_pairs={{0,8},{1,9},{2,10},{3,11},{4,12},{5,13},{6,14},{7,15},{8,0},{9,1},... | collective-permute-start | bytes 245768 | tf_op jit(solution)/shard_map/ppermute | solution.py:188
  86.5 5.6 %collective-permute-start.17 = (f32[128,128]{1,0:T(8,128)S(1)}, f32[128,128]{1,0:T(8,128)S(1)}, u32[]{:S(2)}, u32[]{:S(2)}) collective-permute-start(f32[128,128]{1,0:T(8,128)S(1)} %add.26.kept_ref), channel_id=1, source_target_pairs={{0,24},{1,25},{2,26},{3,27},{4,28},{5,29},{6,30},{7,31},{8,16},{9,... | collective-permute-start | bytes 196616 | tf_op jit(solution)/shard_map/ppermute | solution.py:188
  92.1 1.3 collective-permute-start.18
  93.4 3.9 %collective-permute-start.19 = (f32[64,128]{1,0:T(8,128)S(1)}, f32[64,128]{1,0:T(8,128)S(1)}, u32[]{:S(2)}, u32[]{:S(2)}) collective-permute-start(f32[64,128]{1,0:T(8,128)S(1)} %add.28.kept_ref), channel_id=1, source_target_pairs={{0,64},{32,96},{64,0},{96,32},{128,192},{160,224},{192,128},{224,1... | collective-permute-start | bytes 98312 | tf_op jit(solution)/shard_map/ppermute | solution.py:188
  97.3 4.9 %collective-permute-start.20 = (f32[32,128]{1,0:T(8,128)S(1)}, f32[32,128]{1,0:T(8,128)S(1)}, u32[]{:S(2)}, u32[]{:S(2)}) collective-permute-start(f32[32,128]{1,0:T(8,128)S(1)} %add.29), channel_id=1, source_target_pairs={{0,192},{32,224},{64,128},{96,160},{128,64},{160,96},{192,0},{224,... | collective-permute-start | bytes 49160 | tf_op jit(solution)/shard_map/ppermute | solution.py:188
  102.3 11.8 %collective-permute-start.21 = (f32[256,128]{1,0:T(8,128)S(1)}, f32[256,128]{1,0:T(8,128)S(1)}, u32[]{:S(2)}, u32[]{:S(2)}) collective-permute-start(f32[256,128]{1,0:T(8,128)S(1)} %get-tuple-element.54.own), channel_id=1, source_target_pairs={{0,1},{1,0},{2,3},{3,2},{4,5},{5,4},{6,7},{7,6},{8,9},{9,8},{10,11... | collective-permute-start | bytes 393224 | tf_op jit(solution)/shard_map/ppermute | solution.py:188
  104.6 6.6 %collective-permute-start.23 = (f32[192,128]{1,0:T(8,128)S(1)}, f32[192,128]{1,0:T(8,128)S(1)}, u32[]{:S(2)}, u32[]{:S(2)}) collective-permute-start(f32[192,128]{1,0:T(8,128)S(1)} %get-tuple-element.55), channel_id=1, source_target_pairs={{0,3},{1,2},{2,1},{3,0},{4,7},{5,6},{6,5},{7,4},{8,11},{9,10},{10,... | collective-permute-start | bytes 294920 | tf_op jit(solution)/shard_map/ppermute | solution.py:188
  106.7 7.4 %collective-permute-start.22 = (f32[192,128]{1,0:T(8,128)S(1)}, f32[192,128]{1,0:T(8,128)S(1)}, u32[]{:S(2)}, u32[]{:S(2)}) collective-permute-start(f32[192,128]{1,0:T(8,128)S(1)} %get-tuple-element.55), channel_id=1, source_target_pairs={{0,2},{1,3},{2,0},{3,1},{4,6},{5,7},{6,4},{7,5},{8,10},{9,11},{10,... | collective-permute-start | bytes 294920 | tf_op jit(solution)/shard_map/ppermute | solution.py:188
  116.1 12.3 %collective-permute-start.24 = (f32[320,128]{1,0:T(8,128)S(1)}, f32[320,128]{1,0:T(8,128)S(1)}, u32[]{:S(2)}, u32[]{:S(2)}) collective-permute-start(f32[320,128]{1,0:T(8,128)S(1)} %get-tuple-element.57), channel_id=1, source_target_pairs={{0,1},{1,0},{2,3},{3,2},{4,5},{5,4},{6,7},{7,6},{8,9},{9,8},{10,11... | collective-permute-start | bytes 491528 | tf_op jit(solution)/shard_map/ppermute | solution.py:188
  116.2 12.2 %collective-permute-start.25 = (f32[256,128]{1,0:T(8,128)S(1)}, f32[256,128]{1,0:T(8,128)S(1)}, u32[]{:S(2)}, u32[]{:S(2)}) collective-permute-start(f32[256,128]{1,0:T(8,128)S(1)} %get-tuple-element.59), channel_id=1, source_target_pairs={{0,2},{1,3},{2,0},{3,1},{4,6},{5,7},{6,4},{7,5},{8,10},{9,11},{10,... | collective-permute-start | bytes 393224 | tf_op jit(solution)/shard_map/ppermute | solution.py:188
  118.8 9.6 %collective-permute-start.26 = (f32[256,128]{1,0:T(8,128)S(1)}, f32[256,128]{1,0:T(8,128)S(1)}, u32[]{:S(2)}, u32[]{:S(2)}) collective-permute-start(f32[256,128]{1,0:T(8,128)S(1)} %get-tuple-element.60), channel_id=1, source_target_pairs={{0,3},{1,2},{2,1},{3,0},{4,7},{5,6},{6,5},{7,4},{8,11},{9,10},{10,... | collective-permute-start | bytes 393224 | tf_op jit(solution)/shard_map/ppermute | solution.py:188
  128.5 7.0 %collective-permute-start.27 = (f32[192,128]{1,0:T(8,128)S(1)}, f32[192,128]{1,0:T(8,128)S(1)}, u32[]{:S(2)}, u32[]{:S(2)}) collective-permute-start(f32[192,128]{1,0:T(8,128)S(1)} %get-tuple-element.62.kept_ref), channel_id=1, source_target_pairs={{0,6},{1,7},{2,4},{3,5},{4,2},{5,3},{6,0},{7,1},{8,14},{9,15},{10,... | collective-permute-start | bytes 294920 | tf_op jit(solution)/shard_map/ppermute | solution.py:188
  135.5 4.5 %collective-permute-start.28 = (f32[160,128]{1,0:T(8,128)S(1)}, f32[160,128]{1,0:T(8,128)S(1)}, u32[]{:S(2)}, u32[]{:S(2)}) collective-permute-start(f32[160,128]{1,0:T(8,128)S(1)} %add.30.kept_ref), channel_id=1, source_target_pairs={{0,8},{1,9},{2,10},{3,11},{4,12},{5,13},{6,14},{7,15},{8,0},{9,1},... | collective-permute-start | bytes 245768 | tf_op jit(solution)/shard_map/ppermute | solution.py:188
  140.1 5.6 %collective-permute-start.29 = (f32[128,128]{1,0:T(8,128)S(1)}, f32[128,128]{1,0:T(8,128)S(1)}, u32[]{:S(2)}, u32[]{:S(2)}) collective-permute-start(f32[128,128]{1,0:T(8,128)S(1)} %add.31.kept_ref), channel_id=1, source_target_pairs={{0,24},{1,25},{2,26},{3,27},{4,28},{5,29},{6,30},{7,31},{8,16},{9,... | collective-permute-start | bytes 196616 | tf_op jit(solution)/shard_map/ppermute | solution.py:188
  145.6 1.3 collective-permute-start.30
  146.9 3.9 %collective-permute-start.31 = (f32[64,128]{1,0:T(8,128)S(1)}, f32[64,128]{1,0:T(8,128)S(1)}, u32[]{:S(2)}, u32[]{:S(2)}) collective-permute-start(f32[64,128]{1,0:T(8,128)S(1)} %add.33.kept_ref), channel_id=1, source_target_pairs={{0,64},{32,96},{64,0},{96,32},{128,192},{160,224},{192,128},{224,1... | collective-permute-start | bytes 98312 | tf_op jit(solution)/shard_map/ppermute | solution.py:188
  150.9 4.9 %collective-permute-start.32 = (f32[32,128]{1,0:T(8,128)S(1)}, f32[32,128]{1,0:T(8,128)S(1)}, u32[]{:S(2)}, u32[]{:S(2)}) collective-permute-start(f32[32,128]{1,0:T(8,128)S(1)} %add.34), channel_id=1, source_target_pairs={{0,192},{32,224},{64,128},{96,160},{128,64},{160,96},{192,0},{224,... | collective-permute-start | bytes 49160 | tf_op jit(solution)/shard_map/ppermute | solution.py:188
  155.8 11.9 %collective-permute-start.33 = (f32[256,128]{1,0:T(8,128)S(1)}, f32[256,128]{1,0:T(8,128)S(1)}, u32[]{:S(2)}, u32[]{:S(2)}) collective-permute-start(f32[256,128]{1,0:T(8,128)S(1)} %get-tuple-element.63.own), channel_id=1, source_target_pairs={{0,1},{1,0},{2,3},{3,2},{4,5},{5,4},{6,7},{7,6},{8,9},{9,8},{10,11... | collective-permute-start | bytes 393224 | tf_op jit(solution)/shard_map/ppermute | solution.py:188
  158.3 6.6 %collective-permute-start.35 = (f32[192,128]{1,0:T(8,128)S(1)}, f32[192,128]{1,0:T(8,128)S(1)}, u32[]{:S(2)}, u32[]{:S(2)}) collective-permute-start(f32[192,128]{1,0:T(8,128)S(1)} %get-tuple-element.64), channel_id=1, source_target_pairs={{0,3},{1,2},{2,1},{3,0},{4,7},{5,6},{6,5},{7,4},{8,11},{9,10},{10,... | collective-permute-start | bytes 294920 | tf_op jit(solution)/shard_map/ppermute | solution.py:188
  160.2 7.5 %collective-permute-start.34 = (f32[192,128]{1,0:T(8,128)S(1)}, f32[192,128]{1,0:T(8,128)S(1)}, u32[]{:S(2)}, u32[]{:S(2)}) collective-permute-start(f32[192,128]{1,0:T(8,128)S(1)} %get-tuple-element.64), channel_id=1, source_target_pairs={{0,2},{1,3},{2,0},{3,1},{4,6},{5,7},{6,4},{7,5},{8,10},{9,11},{10,... | collective-permute-start | bytes 294920 | tf_op jit(solution)/shard_map/ppermute | solution.py:188
  169.8 12.3 %collective-permute-start.36 = (f32[320,128]{1,0:T(8,128)S(1)}, f32[320,128]{1,0:T(8,128)S(1)}, u32[]{:S(2)}, u32[]{:S(2)}) collective-permute-start(f32[320,128]{1,0:T(8,128)S(1)} %get-tuple-element.66), channel_id=1, source_target_pairs={{0,1},{1,0},{2,3},{3,2},{4,5},{5,4},{6,7},{7,6},{8,9},{9,8},{10,11... | collective-permute-start | bytes 491528 | tf_op jit(solution)/shard_map/ppermute | solution.py:188
  169.9 12.2 %collective-permute-start.37 = (f32[256,128]{1,0:T(8,128)S(1)}, f32[256,128]{1,0:T(8,128)S(1)}, u32[]{:S(2)}, u32[]{:S(2)}) collective-permute-start(f32[256,128]{1,0:T(8,128)S(1)} %get-tuple-element.68), channel_id=1, source_target_pairs={{0,2},{1,3},{2,0},{3,1},{4,6},{5,7},{6,4},{7,5},{8,10},{9,11},{10,... | collective-permute-start | bytes 393224 | tf_op jit(solution)/shard_map/ppermute | solution.py:188
  172.4 9.7 %collective-permute-start.38 = (f32[256,128]{1,0:T(8,128)S(1)}, f32[256,128]{1,0:T(8,128)S(1)}, u32[]{:S(2)}, u32[]{:S(2)}) collective-permute-start(f32[256,128]{1,0:T(8,128)S(1)} %get-tuple-element.69), channel_id=1, source_target_pairs={{0,3},{1,2},{2,1},{3,0},{4,7},{5,6},{6,5},{7,4},{8,11},{9,10},{10,... | collective-permute-start | bytes 393224 | tf_op jit(solution)/shard_map/ppermute | solution.py:188
  182.1 6.9 %collective-permute-start.39 = (f32[192,128]{1,0:T(8,128)S(1)}, f32[192,128]{1,0:T(8,128)S(1)}, u32[]{:S(2)}, u32[]{:S(2)}) collective-permute-start(f32[192,128]{1,0:T(8,128)S(1)} %get-tuple-element.71.kept_ref), channel_id=1, source_target_pairs={{0,6},{1,7},{2,4},{3,5},{4,2},{5,3},{6,0},{7,1},{8,14},{9,15},{10,... | collective-permute-start | bytes 294920 | tf_op jit(solution)/shard_map/ppermute | solution.py:188
  189.0 4.5 %collective-permute-start.40 = (f32[160,128]{1,0:T(8,128)S(1)}, f32[160,128]{1,0:T(8,128)S(1)}, u32[]{:S(2)}, u32[]{:S(2)}) collective-permute-start(f32[160,128]{1,0:T(8,128)S(1)} %add.35.kept_ref), channel_id=1, source_target_pairs={{0,8},{1,9},{2,10},{3,11},{4,12},{5,13},{6,14},{7,15},{8,0},{9,1},... | collective-permute-start | bytes 245768 | tf_op jit(solution)/shard_map/ppermute | solution.py:188
  193.6 5.6 %collective-permute-start.41 = (f32[128,128]{1,0:T(8,128)S(1)}, f32[128,128]{1,0:T(8,128)S(1)}, u32[]{:S(2)}, u32[]{:S(2)}) collective-permute-start(f32[128,128]{1,0:T(8,128)S(1)} %add.36.kept_ref), channel_id=1, source_target_pairs={{0,24},{1,25},{2,26},{3,27},{4,28},{5,29},{6,30},{7,31},{8,16},{9,... | collective-permute-start | bytes 196616 | tf_op jit(solution)/shard_map/ppermute | solution.py:188
  199.2 1.3 collective-permute-start.42
  200.5 3.9 %collective-permute-start.43 = (f32[64,128]{1,0:T(8,128)S(1)}, f32[64,128]{1,0:T(8,128)S(1)}, u32[]{:S(2)}, u32[]{:S(2)}) collective-permute-start(f32[64,128]{1,0:T(8,128)S(1)} %add.38.kept_ref), channel_id=1, source_target_pairs={{0,64},{32,96},{64,0},{96,32},{128,192},{160,224},{192,128},{224,1... | collective-permute-start | bytes 98312 | tf_op jit(solution)/shard_map/ppermute | solution.py:188
  204.4 4.9 %collective-permute-start.44 = (f32[32,128]{1,0:T(8,128)S(1)}, f32[32,128]{1,0:T(8,128)S(1)}, u32[]{:S(2)}, u32[]{:S(2)}) collective-permute-start(f32[32,128]{1,0:T(8,128)S(1)} %add.39), channel_id=1, source_target_pairs={{0,192},{32,224},{64,128},{96,160},{128,64},{160,96},{192,0},{224,... | collective-permute-start | bytes 49160 | tf_op jit(solution)/shard_map/ppermute | solution.py:188
  209.4 11.9 %collective-permute-start.45 = (f32[256,128]{1,0:T(8,128)S(1)}, f32[256,128]{1,0:T(8,128)S(1)}, u32[]{:S(2)}, u32[]{:S(2)}) collective-permute-start(f32[256,128]{1,0:T(8,128)S(1)} %get-tuple-element.72.refs_1_), channel_id=1, source_target_pairs={{0,1},{1,0},{2,3},{3,2},{4,5},{5,4},{6,7},{7,6},{8,9},{9,8},{10,11... | collective-permute-start | bytes 393224 | tf_op jit(solution)/shard_map/ppermute | solution.py:188
  211.9 6.6 %collective-permute-start.47 = (f32[192,128]{1,0:T(8,128)S(1)}, f32[192,128]{1,0:T(8,128)S(1)}, u32[]{:S(2)}, u32[]{:S(2)}) collective-permute-start(f32[192,128]{1,0:T(8,128)S(1)} %get-tuple-element.73), channel_id=1, source_target_pairs={{0,3},{1,2},{2,1},{3,0},{4,7},{5,6},{6,5},{7,4},{8,11},{9,10},{10,... | collective-permute-start | bytes 294920 | tf_op jit(solution)/shard_map/ppermute | solution.py:188
  213.8 7.5 %collective-permute-start.46 = (f32[192,128]{1,0:T(8,128)S(1)}, f32[192,128]{1,0:T(8,128)S(1)}, u32[]{:S(2)}, u32[]{:S(2)}) collective-permute-start(f32[192,128]{1,0:T(8,128)S(1)} %get-tuple-element.73), channel_id=1, source_target_pairs={{0,2},{1,3},{2,0},{3,1},{4,6},{5,7},{6,4},{7,5},{8,10},{9,11},{10,... | collective-permute-start | bytes 294920 | tf_op jit(solution)/shard_map/ppermute | solution.py:188
